TPU v7x, 1024 devices: a whole 4x4x32 slice. The times are simulated.
1024 devices in a mesh: ctx: 128 (over z, y), chan: 8 (over x, core).
Axes of the slice: x: 4, y: 4, z: 32, core: 2. Of those that a mesh axis runs over, the one named last changes fastest.
Arguments:
- query: bfloat16 [1, 16384, 8192], P(None, 'ctx', 'chan'), may hold values from -6 to 6
- key_in: bfloat16 [1, 16384, 8192], P(None, 'ctx', 'chan'), may hold values from -6 to 6
- value_in: bfloat16 [1, 16384, 8192], P(None, 'ctx', 'chan'), may hold values from -6 to 6
- cotangent: bfloat16 [1, 16384, 8192], P(None, 'ctx', 'chan'), may hold values from -6 to 6
- filters: float32 [512, 128], P('chan'), may hold values from -0.5 to 0.5
- norm_gain: float32 [8192], P('chan'), may hold values from 0.1 to 1.9
Outputs:
- normed: bfloat16 [1, 16384, 8192], P(None, 'ctx', 'chan')
- grad_query: bfloat16 [1, 16384, 8192], P(None, 'ctx', 'chan')
- grad_key: bfloat16 [1, 16384, 8192], P(None, 'ctx', 'chan')
- grad_value: bfloat16 [1, 16384, 8192], P(None, 'ctx', 'chan')
- grad_filters: float32 [512, 128], P('chan')
All inputs are finite; a program needn't handle non-finite values.
Results may differ from a plain program's by a relative error of at most 0.0058.
Values may be sent and summed in bfloat16 or wider, within the bound.
No kernel may reach another device: no remote copies, remote signals or barrier semaphores. Data moves between devices by JAX's collectives and lax.ppermute only.
A program may use at most 64 MiB of HBM per device.

v0:
```python
import functools

import jax
import jax.numpy as jnp
from jax import lax
from jax.sharding import Mesh
from jax.sharding import PartitionSpec as P

D = 8192
CTX = ("ctx_0", "ctx_1")


def shifted(block, axis, distance):
    devices = range(lax.axis_size(axis))
    route = [(i - distance, i) for i in devices if i - distance in devices]
    return lax.ppermute(block, axis, route)


def sent_to_all(x, axis):
    size = lax.axis_size(axis)
    return lax.all_to_all(jnp.broadcast_to(x[None], (size, *x.shape)), axis, 0, 0, tiled=True)


def taken_together(x, axis):
    everything = sent_to_all(x, axis)
    return jnp.sum(everything, axis=0)


def packed_total(arrays, axis):
    ends = [0]
    for a in arrays:
        ends.append(ends[-1] + a.size)
    total = taken_together(jnp.concatenate([a.ravel() for a in arrays]), axis)
    return tuple((total[b:e].reshape(a.shape) for a, b, e in zip(arrays, ends, ends[1:])))


def one_axis_at_a_time(x, axes):
    return functools.reduce(lax.psum, axes, x)


def toeplitz(taps):
    count, width = taps.shape
    zeros = jnp.zeros((count, width), taps.dtype)
    line = jnp.concatenate([zeros, jnp.flip(taps, 1), zeros], axis=1)
    tiled = jnp.tile(line, (1, width))
    tiled = tiled[:, : width * (3 * width - 1)].reshape(count, width, 3 * width - 1)
    return tiled[:, :, width - 1 : 3 * width - 1]


def lag_sums(pairs):
    count, width, double = pairs.shape
    flat = pairs.reshape(count, width * double)
    flat = jnp.concatenate([flat, jnp.zeros((count, width), pairs.dtype)], axis=1)
    skewed = flat.reshape(count, width, double + 1)
    totals = jnp.sum(skewed, axis=1)
    return jnp.flip(totals[:, 1 : width + 1], axis=1)


def channel_major(array, groups):
    batch, length, width = array.shape
    members = width // groups
    moved = array.reshape(batch, length, groups, members).transpose(2, 0, 3, 1)
    return moved.reshape(groups, batch * members, length)


def token_major(array, batch):
    groups, packed, length = array.shape
    members = packed // batch
    moved = array.reshape(groups, batch, members, length).transpose(1, 3, 0, 2)
    return moved.reshape(batch, length, groups * members)


def channel_sum(array, batch):
    groups, packed, length = array.shape
    members = packed // batch
    return jnp.sum(array.reshape(groups, batch, members, length), axis=(0, 2))


def spread(values, groups, members):
    batch, length = values.shape
    wide = jnp.broadcast_to(values[None, :, None, :], (groups, batch, members, length))
    return wide.reshape(groups, batch * members, length)


def body(query, key_in, value_in, cotangent, filters, norm_gain):
    batch, rows, width = query.shape
    groups, taps = filters.shape
    members = width // groups
    packed = batch * members
    blocks_n = rows // taps
    weights = toeplitz(filters.astype(jnp.bfloat16))
    query_cm = channel_major(query, groups)
    key_cm = channel_major(key_in, groups)
    value_cm = channel_major(value_in, groups)
    cotangent_cm = channel_major(cotangent, groups)
    signal = (key_cm.astype(jnp.float32) * value_cm.astype(jnp.float32)).astype(jnp.bfloat16)
    carried = shifted(signal, CTX, 1)
    extent = signal.shape[2] // taps
    blocks = signal.reshape(groups, packed, extent, taps)
    before = jnp.concatenate([carried.reshape(groups, packed, 1, taps), blocks[:, :, :-1]], axis=2)
    window = jnp.concatenate([before, blocks], axis=3)
    mixed = jnp.einsum("gpks,gts->gpkt", window, weights, preferred_element_type=jnp.float32)
    mixed = mixed.reshape(groups, packed, extent * taps)
    gain_cm = norm_gain.reshape(groups, 1, members, 1).reshape(groups, packed, 1)
    lifted = query_cm.astype(jnp.float32) * mixed
    scaled = gain_cm * cotangent_cm.astype(jnp.float32)
    power, inner = packed_total(
        (channel_sum(lifted * lifted, batch), channel_sum(scaled * lifted, batch)), "chan"
    )
    recip = spread(lax.rsqrt(power / D + 1e-06), groups, members)
    inner = spread(inner, groups, members)
    grad_mix = recip * scaled - lifted * recip**3 * inner / D
    grad_conv = (grad_mix * query_cm.astype(jnp.float32)).astype(jnp.bfloat16)
    later = shifted(grad_conv, CTX, -1)
    normed = token_major((lifted * recip * gain_cm).astype(jnp.bfloat16), batch)
    grad_query = token_major((grad_mix * mixed).astype(jnp.bfloat16), batch)
    gathered = jnp.concatenate([grad_conv, later], axis=2).reshape(
        groups, packed, blocks_n + 1, taps
    )
    back = jnp.einsum("gpkt,gts->gpks", gathered, weights, preferred_element_type=jnp.float32)
    grad_signal = (back[:, :, :blocks_n, taps:] + back[:, :, 1:, :taps]).reshape(
        groups, packed, rows
    )
    grad_key = token_major((grad_signal * value_cm.astype(jnp.float32)).astype(jnp.bfloat16), batch)
    grad_value = token_major((grad_signal * key_cm.astype(jnp.float32)).astype(jnp.bfloat16), batch)
    own_blocks = grad_conv.reshape(groups, packed, blocks_n, taps)
    pairs = jnp.einsum("gpkt,gpks->gts", own_blocks, window, preferred_element_type=jnp.float32)
    grad_filters = one_axis_at_a_time(lag_sums(pairs), CTX)
    return (normed, grad_query, grad_key, grad_value, grad_filters)


def solution(mesh):
    torus = Mesh(mesh.devices.reshape(32, 4, mesh.shape["chan"]), ("ctx_0", "ctx_1", "chan"))
    in_specs = (
        P(None, CTX, "chan"),
        P(None, CTX, "chan"),
        P(None, CTX, "chan"),
        P(None, CTX, "chan"),
        P("chan", None),
        P("chan"),
    )
    out_specs = (
        P(None, CTX, "chan"),
        P(None, CTX, "chan"),
        P(None, CTX, "chan"),
        P(None, CTX, "chan"),
        P("chan", None),
    )
    return jax.shard_map(body, mesh=torus, in_specs=in_specs, out_specs=out_specs, check_vma=False)
```

profile of v0, /device:TPU:2, one launch (start us, length us, event | category | flops | bytes accessed | tf_op | source)
XLA Modules:
  0.0 236.7 jit_solution(8800814874270927431)
XLA Ops:
  0.6 1.1 multiply_convert_fusion.5
  1.7 0.2 copy.42
  1.9 3.5 %collective-permute-start = (bf16[64,16,128]{2,1,0:T(8,128)(2,1)S(1)}, bf16[64,16,128]{2,1,0:T(8,128)(2,1)S(1)}, u32[]{:S(2)}, u32[]{:S(2)}) collective-permute-start(bf16[64,16,128]{2,1,0:T(8,128)(2,1)S(1)} %bitcast.77), channel_id=1, source_target_pairs={{0,8},{8,16},{16,24},{24,32},{32,40},{40,48},{48,56},{56,64},{64,7... | collective-permute-start | bytes 786440 | tf_op jit(solution)/shard_map/ppermute | solution.py:16
  5.4 0.8 convert_element_type.124
  6.2 0.1 rev.8
  6.3 0.8 mul.73
  7.0 1.1 copy.41
  8.1 1.1 copy.43
  9.2 0.5 tile.4
  9.8 4.1 %copy.57 = bf16[8,8,128,384]{3,1,2,0:T(8,128)(2,1)S(1)} copy(bf16[8,8,128,384]{3,2,1,0:T(8,128)(2,1)S(1)} %bitcast.71) | data formatting | bytes 12582912
  13.9 3.1 %slice.28 = bf16[64,49024]{1,0:T(8,128)(2,1)} slice(bf16[64,49152]{1,0:T(8,128)(2,1)S(1)} %bitcast.72), slice={[0:64], [0:49024]} | slice | bytes 12550144 | tf_op jit(solution)/shard_map/slice | solution.py:46
  16.9 16.4 %reshape.163 = bf16[64,128,383]{2,1,0:T(8,128)(2,1)} reshape(bf16[64,49024]{1,0:T(8,128)(2,1)} %slice.28) | data formatting | bytes 12550144 | tf_op jit(solution)/shard_map/reshape | solution.py:46
  33.4 0.0 copy-start
  33.4 0.0 copy-start.1
  33.4 0.0 collective-permute-done
  33.4 0.0 copy-start.2
  33.4 5.2 %multiply_reduce_fusion.1 = (f32[128]{0:T(128)S(1)}, f32[128]{0:T(128)S(1)}, f32[64,16,128]{2,1,0:T(8,128)S(1)}, f32[64,16,128]{2,1,0:T(8,128)}) fusion(f32[64,16,128]{2,1,0:T(8,128)S(1)} %bitcast.75, f32[64,16]{1,0:T(8,128)S(1)} %mul.73, f32[64,16,128]{2,1,0:T(8,128)S(1)} %bitcast.73, bf16[64,128,383]{2,1,0:T(8,128)(2,1)} %reshape.163, ...), kind=kOutput, calls=%fused_computation.18 | convolution fusion | flops 68943616 | bytes 6820864 | tf_op jit(solution)/shard_map/gpks,gts->gpkt/dot_general | solution.py:102
  38.6 0.6 broadcast_in_dim.5
  39.2 0.0 copy-done.2
  39.2 14.2 %all-to-all-start = ((f32[8,1,256]{2,1,0:T(1,128)}), f32[8,1,256]{2,1,0:T(1,128)S(1)}, u32[]{:S(2)}, u32[]{:S(2)}) async-start(f32[8,1,256]{2,1,0:T(1,128)} %broadcast_in_dim.5), calls=%async_computation | async-start | bytes 16384 | tf_op jit(solution)/shard_map/all_to_all | solution.py:21
  53.4 0.0 copy-done
  53.4 0.1 copy.47
  53.5 0.0 copy-done.1
  53.5 0.1 copy.46
  53.7 3.6 %all-to-all-done = f32[8,1,256]{2,1,0:T(1,128)S(1)} async-done(((f32[8,1,256]{2,1,0:T(1,128)}), f32[8,1,256]{2,1,0:T(1,128)S(1)}, u32[]{:S(2)}, u32[]{:S(2)}) %all-to-all-start) | async-done | bytes 8224 | tf_op jit(solution)/shard_map/all_to_all | solution.py:21
  57.3 2.0 multiply_convert_fusion.2
  59.3 0.0 copy-start.3
  59.3 1.6 collective-permute-start.1
  60.9 5.5 %fusion.8 = f32[64,128,256]{2,1,0:T(8,128)} fusion(bf16[64,16,128]{2,1,0:T(8,128)(2,1)S(1)} %get-tuple-element.32, bf16[64,16,1,128]{3,1,0,2:T(8,128)(2,1)S(1)} %bitcast.79, bf16[64,16,1,128]{3,1,0,2:T(8,128)(2,1)} %bitcast.83), kind=kOutput, calls=%fused_computation.20 | convolution fusion | flops 68157440 | bytes 9175040 | tf_op jit(solution)/shard_map/gpkt,gpks->gts/dot_general | solution.py:127
  66.4 0.0 copy-done.3
  66.4 0.8 copy.49
  67.3 0.8 copy.48
  68.1 8.1 %copy.58 = f32[8,8,128,256]{3,1,2,0:T(8,128)S(1)} copy(f32[8,8,128,256]{3,2,1,0:T(8,128)} %bitcast.70) | data formatting | bytes 16777216
  76.2 3.8 %concatenate.19 = f32[64,32896]{1,0:T(8,128)} pad(f32[64,32768]{1,0:T(8,128)S(1)} %bitcast.69, f32[]{:T(128)} %constant.5.clone.1), padding=0_0x0_128 | pad | bytes 16809988 | tf_op jit(solution)/shard_map/concatenate | solution.py:53
  80.0 14.1 %reshape.176 = f32[64,128,257]{2,1,0:T(8,128)} reshape(f32[64,32896]{1,0:T(8,128)} %concatenate.19) | data formatting | bytes 16842752 | tf_op jit(solution)/shard_map/reshape | solution.py:54
  94.1 6.1 %reduce_sum.39 = f32[64,257]{1,0:T(8,128)S(1)} reduce(f32[64,128,257]{2,1,0:T(8,128)} %reshape.176, f32[]{:T(128)} %constant.5.clone.1), dimensions={1}, to_apply=%region_3.4 | reduce | flops 2088896 | bytes 8487172 | tf_op jit(solution)/shard_map/reduce_sum | solution.py:55
  100.2 0.1 slice.32
  100.3 0.1 rev.9
  100.4 114.4 %psum.14 = f32[64,128]{1,0:T(8,128)S(1)} all-reduce(f32[64,128]{1,0:T(8,128)S(1)} %rev.9), channel_id=1, replica_groups=mesh['ctx_0'=32,'ctx_1'=4,'chan'=8] {'ctx_0'}, use_global_device_ids=true, to_apply=%region_4.5 | all-reduce | flops 8192 | bytes 65536 | tf_op jit(solution)/shard_map/psum | solution.py:38
  214.8 15.8 %psum.15 = f32[64,128]{1,0:T(8,128)} all-reduce(f32[64,128]{1,0:T(8,128)S(1)} %psum.14), channel_id=1, replica_groups=mesh['ctx_0'=32,'ctx_1'=4,'chan'=8] {'ctx_1'}, use_global_device_ids=true, to_apply=%region_5.6 | all-reduce | flops 8192 | bytes 65536 | tf_op jit(solution)/shard_map/psum | solution.py:38
  230.6 0.0 collective-permute-done.1
  230.6 4.2 %fusion = f32[64,16,2,256]{3,1,2,0:T(8,128)S(1)} fusion(bf16[64,128,383]{2,1,0:T(8,128)(2,1)} %reshape.163, bf16[64,16,128]{2,1,0:T(8,128)(2,1)S(1)} %collective-permute-done.1, bf16[64,16,128]{2,1,0:T(8,128)(2,1)S(1)} %get-tuple-element.32), kind=kOutput, calls=%fused_computation | convolution fusion | flops 135266304 | bytes 6815744 | tf_op jit(solution)/shard_map/gpkt,gts->gpks/dot_general | solution.py:120
  234.8 0.2 multiply_convert_fusion
  235.0 0.9 copy.51
  235.8 0.8 copy.50
  (5 shorter events, 0.1 us)
Async XLA Ops:
  1.9 31.5 %collective-permute-start = (bf16[64,16,128]{2,1,0:T(8,128)(2,1)S(1)}, bf16[64,16,128]{2,1,0:T(8,128)(2,1)S(1)}, u32[]{:S(2)}, u32[]{:S(2)}) collective-permute-start(bf16[64,16,128]{2,1,0:T(8,128)(2,1)S(1)} %bitcast.77), channel_id=1, source_target_pairs={{0,8},{8,16},{16,24},{24,32},{32,40},{40,48},{48,56},{56,64},{64,7... | collective-permute-start | bytes 786440 | tf_op jit(solution)/shard_map/ppermute | solution.py:16
  33.4 20.0 %copy-start = (bf16[1,128,1024]{2,1,0:T(8,128)(2,1)S(1)}, bf16[1,128,1024]{2,1,0:T(8,128)(2,1)}, u32[]{:S(2)}) copy-start(bf16[1,128,1024]{2,1,0:T(8,128)(2,1)} %param.7) | copy-start | bytes 786436
  33.4 20.2 %copy-start.1 = (bf16[1,128,1024]{2,1,0:T(8,128)(2,1)S(1)}, bf16[1,128,1024]{2,1,0:T(8,128)(2,1)}, u32[]{:S(2)}) copy-start(bf16[1,128,1024]{2,1,0:T(8,128)(2,1)} %param.8) | copy-start | bytes 786436
  33.4 5.8 %copy-start.2 = (bf16[64,16,128]{2,1,0:T(8,128)(2,1)}, bf16[64,16,128]{2,1,0:T(8,128)(2,1)S(1)}, u32[]{:S(2)}) copy-start(bf16[64,16,128]{2,1,0:T(8,128)(2,1)S(1)} %collective-permute-done) | copy-start | bytes 786436
  39.2 18.1 %all-to-all-start = ((f32[8,1,256]{2,1,0:T(1,128)}), f32[8,1,256]{2,1,0:T(1,128)S(1)}, u32[]{:S(2)}, u32[]{:S(2)}) async-start(f32[8,1,256]{2,1,0:T(1,128)} %broadcast_in_dim.5), calls=%async_computation | async-start | bytes 16384 | tf_op jit(solution)/shard_map/all_to_all | solution.py:21
  59.3 7.1 %copy-start.3 = (bf16[64,16,128]{2,1,0:T(8,128)(2,1)S(1)}, bf16[64,16,128]{2,1,0:T(8,128)(2,1)}, u32[]{:S(2)}) copy-start(bf16[64,16,128]{2,1,0:T(8,128)(2,1)} %get-tuple-element.33) | copy-start | bytes 786436
  59.3 171.3 %collective-permute-start.1 = (bf16[64,16,128]{2,1,0:T(8,128)(2,1)S(1)}, bf16[64,16,128]{2,1,0:T(8,128)(2,1)S(1)}, u32[]{:S(2)}, u32[]{:S(2)}) collective-permute-start(bf16[64,16,128]{2,1,0:T(8,128)(2,1)S(1)} %get-tuple-element.32), channel_id=1, source_target_pairs={{8,0},{16,8},{24,16},{32,24},{40,32},{48,40},{56,48},{64,56},{72,6... | collective-permute-start | bytes 786440 | tf_op jit(solution)/shard_map/ppermute | solution.py:16
where the time goes:
time: 238 us; the launch traced here: 237 us
  blocking collectives  130 us (55%)
  local copies, waits for them, and re-layouts  57.7 us (24%)
  starting transfers between devices  19.3 us (8%)
  matrix products  14.8 us (6%)
  other arithmetic  10.2 us (4%)
  waiting for transfers between devices  3.6 us (2%)
    psum x2, blocking collectives, one_axis_at_a_time(): return functools.reduce(lax.psum, axes, x)  130 us
    reshape x1, local copies, waits for them, and re-layouts, toeplitz(): tiled[:, :width * (3 * width - 1)].reshape(count, width, 3 * width - 1)  16.4 us
    unnamed x14, local copies, waits for them, and re-layouts  15.6 us
    all_to_all x1, starting transfers between devices, sent_to_all(): lax.all_to_all(jnp.broadcast_to(x[None], (size, *x.shape)), axis, 0, 0, t...  14.2 us
    reshape x1, local copies, waits for them, and re-layouts, lag_sums(): skewed = flat.reshape(count, width, double + 1)  14.1 us
    reduce_sum x1, other arithmetic, lag_sums(): totals = jnp.sum(skewed, axis=1)  6.09 us
    dot_general x1, matrix products, body(): jnp.einsum('gpkt,gpks->gts', own_blocks, window, preferred_element_type=j...  5.47 us
    dot_general x1, matrix products, body(): jnp.einsum('gpks,gts->gpkt', window, weights, preferred_element_type=jnp....  5.18 us
  transfers between devices with their start and end apart: 3, of which 1 were waited for; matrix products, arithmetic and copies ran while one was open for 29% of the time, Pallas kernels for 0%

commit v1 on v0

v1 whole, which is shorter than its diff:
```python
import functools

import jax
import jax.numpy as jnp
from jax import lax
from jax.experimental import pallas as pl
from jax.experimental.pallas import tpu as pltpu
from jax.sharding import Mesh
from jax.sharding import PartitionSpec as P

D = 8192
CTX = ("zh", "zl", "y")
NEAR = ("zl", "y")
FAR = "zh"
LANES = 128
F32 = jnp.float32
BF16 = jnp.bfloat16


def shifted(block, axes, distance):
    devices = range(lax.axis_size(axes))
    route = [(i - distance, i) for i in devices if i - distance in devices]
    return lax.ppermute(block, axes, route)


def exchanged(x, axes):
    return lax.all_to_all(x, axes, 0, 0, tiled=True)


def call(kernel, outs, *args, flops=0, scratch=()):
    moved = sum(a.size * a.dtype.itemsize for a in args)
    moved += sum(o.size * o.dtype.itemsize for o in outs)
    vmem = pl.BlockSpec(memory_space=pltpu.VMEM)
    return pl.pallas_call(
        kernel,
        out_shape=outs,
        in_specs=[vmem] * len(args),
        out_specs=[vmem] * len(outs),
        scratch_shapes=scratch,
        cost_estimate=pl.CostEstimate(flops=flops, bytes_accessed=moved, transcendentals=0),
    )(*args)


def shaped(shape, dtype):
    return jax.ShapeDtypeStruct(shape, dtype)


def rolled(row, taps, shift=0):
    full = jnp.broadcast_to(row, (taps, row.shape[1]))
    return pltpu.roll(full, shift, 1, stride=1, stride_axis=0)


def index(shape, dim):
    return lax.broadcasted_iota(jnp.int32, shape, dim)


def column(row, taps):
    return jnp.broadcast_to(row, (taps, taps)).T


def lane_total(x):
    parts = [x[:, i : i + LANES] for i in range(0, x.shape[1], LANES)]
    while len(parts) > 1:
        parts = [a + b for a, b in zip(parts[::2], parts[1::2])]
    return jnp.sum(parts[0].T, axis=0, keepdims=True)


def signal_kernel(key_ref, value_ref, signal_ref):
    signal_ref[...] = (key_ref[...].astype(F32) * value_ref[...].astype(F32)).astype(BF16)


def weights_kernel(back_taps_ref, signal_ref, weights_ref, mirror_ref):
    groups, taps = back_taps_ref.shape
    row, col = index((taps, taps), 0), index((taps, taps), 1)
    own = row >= col

    def step(g, _):
        c = rolled(back_taps_ref[pl.ds(g, 1), :], taps)
        weights_ref[g, :, :taps] = jnp.where(own, 0.0, c).astype(BF16)
        weights_ref[g, :, taps:] = jnp.where(own, c, 0.0).astype(BF16)
        return 0

    lax.fori_loop(0, groups, step, 0, unroll=4)
    swap = (row + col == taps - 1).astype(BF16)
    mirror_ref[...] = jnp.dot(swap, signal_ref[...], preferred_element_type=F32).astype(BF16)


def mix_kernel(weights_ref, before_ref, signal_ref, query_ref, cot_ref, gain_ref, mixed_ref, sums_ref):
    groups, taps, _ = weights_ref.shape
    width = signal_ref.shape[1]
    per_tile = groups * LANES // width
    members = LANES // per_tile
    owner = index((taps, LANES), 1) // members

    def step(i, totals):
        lanes = pl.ds(pl.multiple_of(i * LANES, LANES), LANES)
        window = jnp.concatenate([before_ref[:, lanes], signal_ref[:, lanes]], axis=0)
        acc = None
        for k in range(per_tile):
            out = jnp.dot(weights_ref[i * per_tile + k], window, preferred_element_type=F32)
            acc = out if acc is None else jnp.where(owner == k, out, acc)
        mixed_ref[:, lanes] = acc
        lifted = query_ref[:, lanes].astype(F32) * acc
        scaled = gain_ref[:, lanes] * cot_ref[:, lanes].astype(F32)
        return totals[0] + lifted * lifted, totals[1] + scaled * lifted

    zero = jnp.zeros((taps, LANES), F32)
    power, inner = lax.fori_loop(0, width // LANES, step, (zero, zero))
    sums = jnp.concatenate(
        [jnp.sum(power.T, axis=0, keepdims=True), jnp.sum(inner.T, axis=0, keepdims=True)], axis=0
    )
    sums_ref[...] = jnp.broadcast_to(sums[None], sums_ref.shape)


def norm_terms(sums_ref, taps):
    sums = jnp.sum(sums_ref[...], axis=0)
    recip = lax.rsqrt(sums[0:1] / D + 1e-6)
    pull = recip * recip * recip * sums[1:2] / D
    return column(recip, taps), column(pull, taps)


def grad_kernel(sums_ref, mixed_ref, query_ref, cot_ref, gain_ref, conv_ref):
    taps, width = mixed_ref.shape
    recip, pull = norm_terms(sums_ref, taps)
    for i in range(0, width, LANES):
        lanes = slice(i, i + LANES)
        query = query_ref[:, lanes].astype(F32)
        scaled = gain_ref[:, lanes] * cot_ref[:, lanes].astype(F32)
        grad_mix = recip * scaled - query * mixed_ref[:, lanes] * pull
        conv_ref[:, lanes] = (grad_mix * query).astype(BF16)


def filter_kernel(conv_ref, before_ref, mirror_ref, totals_ref):
    taps, width = conv_ref.shape
    pieces, per_piece, _ = totals_ref.shape
    groups = pieces * per_piece
    per_tile = groups * LANES // width
    members = LANES // per_tile
    row, col = index((taps, taps), 0), index((taps, taps), 1)
    own = row + col >= taps - 1
    swap = (row + col == taps - 1).astype(BF16)
    owner = col // members

    def step(i, _):
        lanes = pl.ds(pl.multiple_of(i * LANES, LANES), LANES)
        conv = conv_ref[:, lanes]
        past = jnp.dot(swap, before_ref[:, lanes], preferred_element_type=F32).astype(BF16)
        window = jnp.concatenate([past, mirror_ref[:, lanes]], axis=0)
        found = []
        for k in range(per_tile):
            mine = jnp.where(owner == k, conv, jnp.zeros_like(conv))
            pairs = lax.dot_general(
                mine, window, (((1,), (1,)), ((), ())), preferred_element_type=F32
            )
            both = jnp.where(own, pairs[:, taps:], pairs[:, :taps])
            lined = pltpu.roll(both, 1, 1, stride=1, stride_axis=0)
            found.append(jnp.sum(lined, axis=0, keepdims=True))
        for k in range(0, per_tile, per_piece):
            totals_ref[i * (per_tile // per_piece) + k // per_piece] = jnp.concatenate(
                found[k : k + per_piece], axis=0
            )
        return 0

    lax.fori_loop(0, width // LANES, step, 0)


def output_kernel(sums_ref, mixed_ref, query_ref, cot_ref, gain_ref, normed_ref, query_grad_ref):
    taps, width = mixed_ref.shape
    recip, pull = norm_terms(sums_ref, taps)
    for i in range(0, width, LANES):
        lanes = slice(i, i + LANES)
        mixed = mixed_ref[:, lanes]
        lifted = query_ref[:, lanes].astype(F32) * mixed
        scaled = gain_ref[:, lanes] * cot_ref[:, lanes].astype(F32)
        normed_ref[:, lanes] = (lifted * recip * gain_ref[:, lanes]).astype(BF16)
        query_grad_ref[:, lanes] = ((recip * scaled - lifted * pull) * mixed).astype(BF16)


def back_kernel(taps_ref, conv_ref, after_ref, key_ref, value_ref, key_grad_ref, value_grad_ref):
    groups, taps = taps_ref.shape
    width = conv_ref.shape[1]
    per_tile = groups * LANES // width
    members = LANES // per_tile
    row, col = index((taps, taps), 0), index((taps, taps), 1)
    own = col >= row
    owner = col // members

    def step(i, _):
        lanes = pl.ds(pl.multiple_of(i * LANES, LANES), LANES)
        window = jnp.concatenate([conv_ref[:, lanes], after_ref[:, lanes]], axis=0)
        acc = None
        for k in range(per_tile):
            c = rolled(taps_ref[pl.ds(i * per_tile + k, 1), :], taps)
            weights = jnp.concatenate(
                [jnp.where(own, c, 0.0).astype(BF16), jnp.where(own, 0.0, c).astype(BF16)], axis=1
            )
            out = jnp.dot(weights, window, preferred_element_type=F32)
            acc = out if acc is None else jnp.where(owner == k, out, acc)
        key_grad_ref[:, lanes] = (acc * value_ref[:, lanes].astype(F32)).astype(BF16)
        value_grad_ref[:, lanes] = (acc * key_ref[:, lanes].astype(F32)).astype(BF16)
        return 0

    lax.fori_loop(0, width // LANES, step, 0)


def gather_sum_kernel(parts_ref, out_ref):
    out_ref[...] = jnp.broadcast_to(jnp.sum(parts_ref[...], axis=0)[None], out_ref.shape)


def body(query, key_in, value_in, cotangent, filters, norm_gain):
    _, taps, width = query.shape
    groups = filters.shape[0]
    query, key_in, value_in, cotangent = (
        a.reshape(taps, width) for a in (query, key_in, value_in, cotangent)
    )
    gain = norm_gain.reshape(1, width)
    rounded = filters.astype(BF16).astype(F32)
    back_taps = jnp.roll(jnp.flip(rounded, 1), 1, axis=1)
    block = shaped((taps, width), BF16)
    peers = lax.axis_size("chan")
    near, far = lax.axis_size(NEAR), lax.axis_size(FAR)
    conv_flops = 4 * groups * taps * taps * LANES

    (signal,) = call(signal_kernel, [block], key_in, value_in)
    before = shifted(signal, CTX, 1)
    weights, mirror = call(
        weights_kernel, [shaped((groups, taps, 2 * taps), BF16), block], back_taps, signal
    )
    mixed, sums = call(
        mix_kernel,
        [shaped((taps, width), F32), shaped((peers, 2, taps), F32)],
        weights, before, signal, query, cotangent, gain,
        flops=conv_flops,
    )
    sums = exchanged(sums, "chan")
    (conv,) = call(grad_kernel, [block], sums, mixed, query, cotangent, gain)
    (totals,) = call(
        filter_kernel, [shaped((near, groups // near, taps), F32)], conv, before, mirror,
        flops=conv_flops,
    )
    totals = exchanged(totals, NEAR)
    after = shifted(conv, CTX, -1)
    normed, grad_query = call(
        output_kernel, [block, block], sums, mixed, query, cotangent, gain
    )
    (totals,) = call(
        gather_sum_kernel, [shaped((far, groups // near, taps), F32)], totals
    )
    totals = exchanged(totals, FAR)
    grad_key, grad_value = call(
        back_kernel, [block, block], rounded, conv, after, key_in, value_in, flops=conv_flops
    )
    (totals,) = call(
        gather_sum_kernel, [shaped((near, groups // near, taps), F32)], totals
    )
    grad_filters = exchanged(totals, NEAR).reshape(groups, taps)
    return tuple(a[None] for a in (normed, grad_query, grad_key, grad_value)) + (grad_filters,)


def solution(mesh):
    torus = Mesh(
        mesh.devices.reshape(8, 4, 4, mesh.shape["chan"]), ("zh", "zl", "y", "chan")
    )
    rows = P(None, CTX, "chan")
    in_specs = (rows, rows, rows, rows, P("chan", None), P("chan"))
    out_specs = (rows, rows, rows, rows, P("chan", None))
    return jax.shard_map(body, mesh=torus, in_specs=in_specs, out_specs=out_specs, check_vma=False)
```

time: 238 us -> 119 us (0.50)
  the two profiles are of different devices: /device:TPU:2 before, /device:TPU:8 now
where the time goes in v1:
time: 119 us; the launch traced here: 118 us
  starting transfers between devices  33.4 us (28%)
  Pallas kernels  30 us (25%)
  waiting for transfers between devices  27.8 us (23%)
  blocking collectives  22.1 us (19%)
  local copies, waits for them, and re-layouts  2.77 us (2%)
  other arithmetic  1.47 us (1%)
    pallas_call x9, Pallas kernels, call(): pl.pallas_call(kernel, out_shape=outs, in_specs=[vmem] * len(args), out_s...  30 us
    all_to_all x2, starting transfers between devices, exchanged(): return lax.all_to_all(x, axes, 0, 0, tiled=True)  26.6 us
    all_to_all x2, blocking collectives, exchanged(): return lax.all_to_all(x, axes, 0, 0, tiled=True)  22.1 us
    all_to_all x2, waiting for transfers between devices, exchanged(): return lax.all_to_all(x, axes, 0, 0, tiled=True)  18.8 us
    ppermute x2, waiting for transfers between devices, shifted(): return lax.ppermute(block, axes, route)  8.93 us
    ppermute x2, starting transfers between devices, shifted(): return lax.ppermute(block, axes, route)  6.82 us
    unnamed x9, local copies, waits for them, and re-layouts  2.63 us
  transfers between devices with their start and end apart: 4, of which 2 were waited for; matrix products, arithmetic and copies ran while one was open for 1% of the time, Pallas kernels for 11%

profile of v1, /device:TPU:8, one launch (start us, length us, event | category | flops | bytes accessed | tf_op | source)
XLA Modules:
  0.0 118.1 jit_solution(6654099433599790629)
XLA Ops:
  0.6 1.8 %shard_map.101.signal_ref = bf16[128,1024]{1,0:T(8,128)(2,1)} custom-call(bf16[128,1024]{1,0:T(8,128)(2,1)} %bitcast.18, bf16[128,1024]{1,0:T(8,128)(2,1)} %bitcast.20), custom_call_target="tpu_custom_call" | custom-call | bytes 786432 | tf_op jit(solution)/shard_map/pallas_call | solution.py:34
  2.4 3.5 %collective-permute-start = (bf16[128,1024]{1,0:T(8,128)(2,1)}, bf16[128,1024]{1,0:T(8,128)(2,1)S(1)}, u32[]{:S(2)}, u32[]{:S(2)}) collective-permute-start(bf16[128,1024]{1,0:T(8,128)(2,1)} %shard_map.101.signal_ref), channel_id=1, source_target_pairs={{0,8},{8,16},{16,24},{24,32},{32,40},{40,48},{48,56},{56,64},{64,7... | collective-permute-start | bytes 786440 | tf_op jit(solution)/shard_map/ppermute | solution.py:23
  5.9 0.8 convert_convert_fusion.taps_ref
  6.7 0.0 copy-start
  6.7 0.1 slice.16
  6.7 0.1 slice.14
  6.8 0.7 pad_maximum_fusion.back_taps_ref
  7.5 4.9 %shard_map.102 = (bf16[64,128,256]{2,1,0:T(8,128)(2,1)}, bf16[128,1024]{1,0:T(8,128)(2,1)}) custom-call(f32[64,128]{1,0:T(8,128)} %pad_maximum_fusion.back_taps_ref, bf16[128,1024]{1,0:T(8,128)(2,1)} %shard_map.101.signal_ref), custom_call_target="tpu_custom_call" | custom-call | bytes 4751360 | tf_op jit(solution)/shard_map/pallas_call | solution.py:34
  12.4 8.9 %collective-permute-done.before_ref = bf16[128,1024]{1,0:T(8,128)(2,1)S(1)} collective-permute-done((bf16[128,1024]{1,0:T(8,128)(2,1)}, bf16[128,1024]{1,0:T(8,128)(2,1)S(1)}, u32[]{:S(2)}, u32[]{:S(2)}) %collective-permute-start) | collective-permute-done | bytes 262176 | tf_op jit(solution)/shard_map/ppermute | solution.py:23
  21.3 0.0 copy-start.1
  21.3 0.7 copy-done.1
  22.0 5.6 %shard_map.103 = (f32[128,1024]{1,0:T(8,128)}, f32[8,2,128]{2,1,0:T(2,128)}) custom-call(bf16[64,128,256]{2,1,0:T(8,128)(2,1)} %get-tuple-element.13.weights_ref, bf16[128,1024]{1,0:T(8,128)(2,1)} %copy-done.1, bf16[128,1024]{1,0:T(8,128)(2,1)} %shard_map.101.signal_ref, bf16[128,1024]{1,0:T(8,128)(2,1)} %bitcast.11, bf16[128,1024]{1,0:T(8,128)(2,1)} %bitcast.14, ...), custom_call_target="tpu_custom_call" | custom-call | flops 536870912 | bytes 5779456 | tf_op jit(solution)/shard_map/pallas_call | solution.py:34
  27.6 9.2 %all_to_all.20.sums_ref = f32[8,2,128]{2,1,0:T(2,128)} all-to-all(f32[8,2,128]{2,1,0:T(2,128)} %get-tuple-element.14), channel_id=1, replica_groups=mesh['zh'=8,'zl'=4,'y'=4,'chan'=8] {'chan'}, dimensions={0} | all-to-all | bytes 16384 | tf_op jit(solution)/shard_map/all_to_all | solution.py:27
  36.9 2.1 %shard_map.105.conv_ref = bf16[128,1024]{1,0:T(8,128)(2,1)} custom-call(f32[8,2,128]{2,1,0:T(2,128)} %all_to_all.20.sums_ref, f32[128,1024]{1,0:T(8,128)} %get-tuple-element.15.mixed_ref, bf16[128,1024]{1,0:T(8,128)(2,1)} %bitcast.12, bf16[128,1024]{1,0:T(8,128)(2,1)} %bitcast.15, f32[1,1024]{1,0:T(1,128)} %bitcast.24), custom_call_target="tpu_custom_call" | custom-call | bytes 1323008 | tf_op jit(solution)/shard_map/pallas_call | solution.py:34
  39.0 5.9 %shard_map.107 = f32[16,4,128]{2,1,0:T(4,128)} custom-call(bf16[128,1024]{1,0:T(8,128)(2,1)} %shard_map.105.conv_ref, bf16[128,1024]{1,0:T(8,128)(2,1)} %copy-done.1, bf16[128,1024]{1,0:T(8,128)(2,1)} %get-tuple-element.20.mirror_ref), custom_call_target="tpu_custom_call" | custom-call | flops 536870912 | bytes 819200 | tf_op jit(solution)/shard_map/pallas_call | solution.py:34
  44.9 0.0 copy-done
  44.9 12.8 %all_to_all.21.parts_ref = f32[16,4,128]{2,1,0:T(4,128)} all-to-all(f32[16,4,128]{2,1,0:T(4,128)} %shard_map.107), channel_id=1, replica_groups=mesh['zh'=8,'zl'=4,'y'=4,'chan'=8] {'zl','y'}, dimensions={0} | all-to-all | bytes 65536 | tf_op jit(solution)/shard_map/all_to_all | solution.py:27
  57.7 1.4 %shard_map.108 = f32[8,4,128]{2,1,0:T(4,128)} custom-call(f32[16,4,128]{2,1,0:T(4,128)} %all_to_all.21.parts_ref), custom_call_target="tpu_custom_call" | custom-call | bytes 49152 | tf_op jit(solution)/shard_map/pallas_call | solution.py:34
  59.1 21.9 %all-to-all-start.2 = ((f32[8,4,128]{2,1,0:T(4,128)}), f32[8,4,128]{2,1,0:T(4,128)S(1)}, u32[]{:S(2)}, u32[]{:S(2)}) async-start(f32[8,4,128]{2,1,0:T(4,128)} %shard_map.108), calls=%async_computation.2 | async-start | bytes 32768 | tf_op jit(solution)/shard_map/all_to_all | solution.py:27
  80.9 3.4 %collective-permute-start.1 = (bf16[128,1024]{1,0:T(8,128)(2,1)}, bf16[128,1024]{1,0:T(8,128)(2,1)S(1)}, u32[]{:S(2)}, u32[]{:S(2)}) collective-permute-start(bf16[128,1024]{1,0:T(8,128)(2,1)} %shard_map.105.conv_ref), channel_id=1, source_target_pairs={{8,0},{16,8},{24,16},{32,24},{40,32},{48,40},{56,48},{64,56},{72,6... | collective-permute-start | bytes 786440 | tf_op jit(solution)/shard_map/ppermute | solution.py:23
  84.3 18.8 %all-to-all-done.2.parts_ref = f32[8,4,128]{2,1,0:T(4,128)S(1)} async-done(((f32[8,4,128]{2,1,0:T(4,128)}), f32[8,4,128]{2,1,0:T(4,128)S(1)}, u32[]{:S(2)}, u32[]{:S(2)}) %all-to-all-start.2) | async-done | bytes 16416 | tf_op jit(solution)/shard_map/all_to_all | solution.py:27
  103.1 0.0 copy-start.2
  103.1 0.6 copy-done.2
  103.7 1.3 %shard_map.109 = f32[16,4,128]{2,1,0:T(4,128)} custom-call(f32[8,4,128]{2,1,0:T(4,128)} %copy-done.2), custom_call_target="tpu_custom_call" | custom-call | bytes 49152 | tf_op jit(solution)/shard_map/pallas_call | solution.py:34
  105.1 4.7 %all-to-all-start.3 = ((f32[16,4,128]{2,1,0:T(4,128)}), f32[16,4,128]{2,1,0:T(4,128)S(1)}, u32[]{:S(2)}, u32[]{:S(2)}) async-start(f32[16,4,128]{2,1,0:T(4,128)} %shard_map.109), calls=%async_computation.3 | async-start | bytes 65536 | tf_op jit(solution)/shard_map/all_to_all | solution.py:27
  109.8 2.2 %shard_map.104 = (bf16[128,1024]{1,0:T(8,128)(2,1)}, bf16[128,1024]{1,0:T(8,128)(2,1)}) custom-call(f32[8,2,128]{2,1,0:T(2,128)} %all_to_all.20.sums_ref, f32[128,1024]{1,0:T(8,128)} %get-tuple-element.15.mixed_ref, bf16[128,1024]{1,0:T(8,128)(2,1)} %bitcast.13, bf16[128,1024]{1,0:T(8,128)(2,1)} %bitcast.16, f32[1,1024]{1,0:T(1,128)} %bitcast.25), custom_call_target="tpu_custom_call" | custom-call | bytes 1585152 | tf_op jit(solution)/shard_map/pallas_call | solution.py:34
  112.0 0.0 collective-permute-done.1.after_ref
  112.0 0.0 copy-start.3
  112.0 0.7 copy-done.3
  112.7 4.8 %shard_map.106 = (bf16[128,1024]{1,0:T(8,128)(2,1)}, bf16[128,1024]{1,0:T(8,128)(2,1)}) custom-call(f32[64,128]{1,0:T(8,128)} %copy-done, bf16[128,1024]{1,0:T(8,128)(2,1)} %shard_map.105.conv_ref, bf16[128,1024]{1,0:T(8,128)(2,1)} %copy-done.3, bf16[128,1024]{1,0:T(8,128)(2,1)} %bitcast.19, bf16[128,1024]{1,0:T(8,128)(2,1)} %bitcast.21), custom_call_target="tpu_custom_call" | custom-call | flops 536870912 | bytes 1605632 | tf_op jit(solution)/shard_map/pallas_call | solution.py:34
  117.5 0.0 all-to-all-done.3
  117.5 0.6 copy.12
Async XLA Ops:
  2.4 18.9 %collective-permute-start = (bf16[128,1024]{1,0:T(8,128)(2,1)}, bf16[128,1024]{1,0:T(8,128)(2,1)S(1)}, u32[]{:S(2)}, u32[]{:S(2)}) collective-permute-start(bf16[128,1024]{1,0:T(8,128)(2,1)} %shard_map.101.signal_ref), channel_id=1, source_target_pairs={{0,8},{8,16},{16,24},{24,32},{32,40},{40,48},{48,56},{56,64},{64,7... | collective-permute-start | bytes 786440 | tf_op jit(solution)/shard_map/ppermute | solution.py:23
  6.7 38.2 %copy-start = (f32[64,128]{1,0:T(8,128)}, f32[64,128]{1,0:T(8,128)S(1)}, u32[]{:S(2)}) copy-start(f32[64,128]{1,0:T(8,128)S(1)} %convert_convert_fusion.taps_ref) | copy-start | bytes 98308
  21.3 0.7 copy-start.1
  59.1 44.0 %all-to-all-start.2 = ((f32[8,4,128]{2,1,0:T(4,128)}), f32[8,4,128]{2,1,0:T(4,128)S(1)}, u32[]{:S(2)}, u32[]{:S(2)}) async-start(f32[8,4,128]{2,1,0:T(4,128)} %shard_map.108), calls=%async_computation.2 | async-start | bytes 32768 | tf_op jit(solution)/shard_map/all_to_all | solution.py:27
  80.9 31.1 %collective-permute-start.1 = (bf16[128,1024]{1,0:T(8,128)(2,1)}, bf16[128,1024]{1,0:T(8,128)(2,1)S(1)}, u32[]{:S(2)}, u32[]{:S(2)}) collective-permute-start(bf16[128,1024]{1,0:T(8,128)(2,1)} %shard_map.105.conv_ref), channel_id=1, source_target_pairs={{8,0},{16,8},{24,16},{32,24},{40,32},{48,40},{56,48},{64,56},{72,6... | collective-permute-start | bytes 786440 | tf_op jit(solution)/shard_map/ppermute | solution.py:23
  103.1 0.6 copy-start.2
  105.1 12.5 %all-to-all-start.3 = ((f32[16,4,128]{2,1,0:T(4,128)}), f32[16,4,128]{2,1,0:T(4,128)S(1)}, u32[]{:S(2)}, u32[]{:S(2)}) async-start(f32[16,4,128]{2,1,0:T(4,128)} %shard_map.109), calls=%async_computation.3 | async-start | bytes 65536 | tf_op jit(solution)/shard_map/all_to_all | solution.py:27
  112.0 0.7 copy-start.3

commit v2 on v1

--- a/solution.py
+++ b/solution.py
@@ -1,5 +1,3 @@
-import functools
-
 import jax
 import jax.numpy as jnp
 from jax import lax
@@ -8,11 +6,13 @@
 from jax.sharding import Mesh
 from jax.sharding import PartitionSpec as P
 
+
 D = 8192
 CTX = ("zh", "zl", "y")
 NEAR = ("zl", "y")
 FAR = "zh"
 LANES = 128
+VMEM_LIMIT = 16 * 2**20
 F32 = jnp.float32
 BF16 = jnp.bfloat16
 
@@ -23,8 +23,8 @@
     return lax.ppermute(block, axes, route)
 
 
-def exchanged(x, axes):
-    return lax.all_to_all(x, axes, 0, 0, tiled=True)
+def exchanged(x, axes, groups=None):
+    return lax.all_to_all(x, axes, 0, 0, axis_index_groups=groups, tiled=True)
 
 
 def call(kernel, outs, *args, flops=0, scratch=()):
@@ -37,6 +37,7 @@
         in_specs=[vmem] * len(args),
         out_specs=[vmem] * len(outs),
         scratch_shapes=scratch,
+        compiler_params=pltpu.CompilerParams(vmem_limit_bytes=VMEM_LIMIT),
         cost_estimate=pl.CostEstimate(flops=flops, bytes_accessed=moved, transcendentals=0),
     )(*args)
 
@@ -58,21 +59,17 @@
     return jnp.broadcast_to(row, (taps, taps)).T
 
 
-def lane_total(x):
-    parts = [x[:, i : i + LANES] for i in range(0, x.shape[1], LANES)]
-    while len(parts) > 1:
-        parts = [a + b for a, b in zip(parts[::2], parts[1::2])]
-    return jnp.sum(parts[0].T, axis=0, keepdims=True)
-
-
-def signal_kernel(key_ref, value_ref, signal_ref):
-    signal_ref[...] = (key_ref[...].astype(F32) * value_ref[...].astype(F32)).astype(BF16)
-
-
-def weights_kernel(back_taps_ref, signal_ref, weights_ref, mirror_ref):
-    groups, taps = back_taps_ref.shape
+def prepare_kernel(
+    filters_ref, signal_ref, query_ref, cot_ref, gain_ref,
+    weights_ref, mirror_ref, held_ref, scaled_ref, back_taps_ref,
+):
+    groups, taps = filters_ref.shape
     row, col = index((taps, taps), 0), index((taps, taps), 1)
     own = row >= col
+    turn = (lax.rem(row + col, taps) == 0).astype(BF16)
+    back_taps_ref[...] = jnp.dot(
+        filters_ref[...].astype(BF16), turn, preferred_element_type=F32
+    )
 
     def step(g, _):
         c = rolled(back_taps_ref[pl.ds(g, 1), :], taps)
@@ -83,9 +80,11 @@
     lax.fori_loop(0, groups, step, 0, unroll=4)
     swap = (row + col == taps - 1).astype(BF16)
     mirror_ref[...] = jnp.dot(swap, signal_ref[...], preferred_element_type=F32).astype(BF16)
-
-
-def mix_kernel(weights_ref, before_ref, signal_ref, query_ref, cot_ref, gain_ref, mixed_ref, sums_ref):
+    held_ref[...] = query_ref[...]
+    scaled_ref[...] = gain_ref[...] * cot_ref[...].astype(F32)
+
+
+def mix_kernel(weights_ref, before_ref, signal_ref, query_ref, scaled_ref, mixed_ref, sums_ref):
     groups, taps, _ = weights_ref.shape
     width = signal_ref.shape[1]
     per_tile = groups * LANES // width
@@ -101,8 +100,7 @@
             acc = out if acc is None else jnp.where(owner == k, out, acc)
         mixed_ref[:, lanes] = acc
         lifted = query_ref[:, lanes].astype(F32) * acc
-        scaled = gain_ref[:, lanes] * cot_ref[:, lanes].astype(F32)
-        return totals[0] + lifted * lifted, totals[1] + scaled * lifted
+        return totals[0] + lifted * lifted, totals[1] + scaled_ref[:, lanes] * lifted
 
     zero = jnp.zeros((taps, LANES), F32)
     power, inner = lax.fori_loop(0, width // LANES, step, (zero, zero))
@@ -119,18 +117,9 @@
     return column(recip, taps), column(pull, taps)
 
 
-def grad_kernel(sums_ref, mixed_ref, query_ref, cot_ref, gain_ref, conv_ref):
-    taps, width = mixed_ref.shape
-    recip, pull = norm_terms(sums_ref, taps)
-    for i in range(0, width, LANES):
-        lanes = slice(i, i + LANES)
-        query = query_ref[:, lanes].astype(F32)
-        scaled = gain_ref[:, lanes] * cot_ref[:, lanes].astype(F32)
-        grad_mix = recip * scaled - query * mixed_ref[:, lanes] * pull
-        conv_ref[:, lanes] = (grad_mix * query).astype(BF16)
-
-
-def filter_kernel(conv_ref, before_ref, mirror_ref, totals_ref):
+def filter_kernel(
+    sums_ref, mixed_ref, query_ref, scaled_ref, before_ref, mirror_ref, conv_ref, totals_ref
+):
     taps, width = conv_ref.shape
     pieces, per_piece, _ = totals_ref.shape
     groups = pieces * per_piece
@@ -140,10 +129,14 @@
     own = row + col >= taps - 1
     swap = (row + col == taps - 1).astype(BF16)
     owner = col // members
+    recip, pull = norm_terms(sums_ref, taps)
 
     def step(i, _):
         lanes = pl.ds(pl.multiple_of(i * LANES, LANES), LANES)
-        conv = conv_ref[:, lanes]
+        query = query_ref[:, lanes].astype(F32)
+        grad_mix = recip * scaled_ref[:, lanes] - query * mixed_ref[:, lanes] * pull
+        conv = (grad_mix * query).astype(BF16)
+        conv_ref[:, lanes] = conv
         past = jnp.dot(swap, before_ref[:, lanes], preferred_element_type=F32).astype(BF16)
         window = jnp.concatenate([past, mirror_ref[:, lanes]], axis=0)
         found = []
@@ -164,20 +157,25 @@
     lax.fori_loop(0, width // LANES, step, 0)
 
 
-def output_kernel(sums_ref, mixed_ref, query_ref, cot_ref, gain_ref, normed_ref, query_grad_ref):
+def output_kernel(
+    sums_ref, mixed_ref, query_ref, scaled_ref, gain_ref, normed_ref, query_grad_ref
+):
     taps, width = mixed_ref.shape
     recip, pull = norm_terms(sums_ref, taps)
     for i in range(0, width, LANES):
         lanes = slice(i, i + LANES)
         mixed = mixed_ref[:, lanes]
         lifted = query_ref[:, lanes].astype(F32) * mixed
-        scaled = gain_ref[:, lanes] * cot_ref[:, lanes].astype(F32)
         normed_ref[:, lanes] = (lifted * recip * gain_ref[:, lanes]).astype(BF16)
-        query_grad_ref[:, lanes] = ((recip * scaled - lifted * pull) * mixed).astype(BF16)
-
-
-def back_kernel(taps_ref, conv_ref, after_ref, key_ref, value_ref, key_grad_ref, value_grad_ref):
-    groups, taps = taps_ref.shape
+        query_grad_ref[:, lanes] = (
+            (recip * scaled_ref[:, lanes] - lifted * pull) * mixed
+        ).astype(BF16)
+
+
+def back_kernel(
+    filters_ref, conv_ref, after_ref, key_ref, value_ref, key_grad_ref, value_grad_ref
+):
+    groups, taps = filters_ref.shape
     width = conv_ref.shape[1]
     per_tile = groups * LANES // width
     members = LANES // per_tile
@@ -190,7 +188,8 @@
         window = jnp.concatenate([conv_ref[:, lanes], after_ref[:, lanes]], axis=0)
         acc = None
         for k in range(per_tile):
-            c = rolled(taps_ref[pl.ds(i * per_tile + k, 1), :], taps)
+            own_taps = filters_ref[pl.ds(i * per_tile + k, 1), :].astype(BF16).astype(F32)
+            c = rolled(own_taps, taps)
             weights = jnp.concatenate(
                 [jnp.where(own, c, 0.0).astype(BF16), jnp.where(own, 0.0, c).astype(BF16)], axis=1
             )
@@ -214,45 +213,49 @@
         a.reshape(taps, width) for a in (query, key_in, value_in, cotangent)
     )
     gain = norm_gain.reshape(1, width)
-    rounded = filters.astype(BF16).astype(F32)
-    back_taps = jnp.roll(jnp.flip(rounded, 1), 1, axis=1)
     block = shaped((taps, width), BF16)
     peers = lax.axis_size("chan")
     near, far = lax.axis_size(NEAR), lax.axis_size(FAR)
     conv_flops = 4 * groups * taps * taps * LANES
 
-    (signal,) = call(signal_kernel, [block], key_in, value_in)
+    signal = (key_in.astype(F32) * value_in.astype(F32)).astype(BF16)
     before = shifted(signal, CTX, 1)
-    weights, mirror = call(
-        weights_kernel, [shaped((groups, taps, 2 * taps), BF16), block], back_taps, signal
+    wide = shaped((taps, width), F32)
+    weights, mirror, held, scaled = call(
+        prepare_kernel,
+        [shaped((groups, taps, 2 * taps), BF16), block, block, wide],
+        filters, signal, query, cotangent, gain,
+        scratch=[pltpu.VMEM((groups, taps), F32)],
     )
     mixed, sums = call(
         mix_kernel,
-        [shaped((taps, width), F32), shaped((peers, 2, taps), F32)],
-        weights, before, signal, query, cotangent, gain,
+        [wide, shaped((peers, 2, taps), F32)],
+        weights, before, signal, held, scaled,
         flops=conv_flops,
     )
     sums = exchanged(sums, "chan")
-    (conv,) = call(grad_kernel, [block], sums, mixed, query, cotangent, gain)
-    (totals,) = call(
-        filter_kernel, [shaped((near, groups // near, taps), F32)], conv, before, mirror,
+    conv, totals = call(
+        filter_kernel,
+        [block, shaped((near, groups // near, taps), F32)],
+        sums, mixed, held, scaled, before, mirror,
         flops=conv_flops,
     )
     totals = exchanged(totals, NEAR)
+    (totals,) = call(gather_sum_kernel, [shaped((far, groups // near, taps), F32)], totals)
+    totals, conv, sums = lax.optimization_barrier((totals, conv, sums))
+    order = [(i + far // 2) % far for i in range(far)]
+    totals = exchanged(totals, FAR, [order])
     after = shifted(conv, CTX, -1)
     normed, grad_query = call(
-        output_kernel, [block, block], sums, mixed, query, cotangent, gain
-    )
-    (totals,) = call(
-        gather_sum_kernel, [shaped((far, groups // near, taps), F32)], totals
-    )
-    totals = exchanged(totals, FAR)
+        output_kernel, [block, block], sums, mixed, held, scaled, gain
+    )
     grad_key, grad_value = call(
-        back_kernel, [block, block], rounded, conv, after, key_in, value_in, flops=conv_flops
-    )
-    (totals,) = call(
-        gather_sum_kernel, [shaped((near, groups // near, taps), F32)], totals
-    )
+        back_kernel, [block, block], filters, conv, after, key_in, value_in, flops=conv_flops
+    )
+    totals, normed, grad_query, grad_key, grad_value = lax.optimization_barrier(
+        (totals, normed, grad_query, grad_key, grad_value)
+    )
+    (totals,) = call(gather_sum_kernel, [shaped((near, groups // near, taps), F32)], totals)
     grad_filters = exchanged(totals, NEAR).reshape(groups, taps)
     return tuple(a[None] for a in (normed, grad_query, grad_key, grad_value)) + (grad_filters,)
 
@@ -264,4 +267,5 @@
     rows = P(None, CTX, "chan")
     in_specs = (rows, rows, rows, rows, P("chan", None), P("chan"))
     out_specs = (rows, rows, rows, rows, P("chan", None))
+
     return jax.shard_map(body, mesh=torus, in_specs=in_specs, out_specs=out_specs, check_vma=False)

time: 119 us -> 95.7 us (0.80)
  the two profiles are of different devices: /device:TPU:8 before, /device:TPU:2 now
where the time goes in v2:
time: 95.7 us; the launch traced here: 95.2 us
  blocking collectives  38.6 us (40%)
  starting transfers between devices  36.6 us (38%)
  Pallas kernels  14.3 us (15%)
  local copies, waits for them, and re-layouts  3.98 us (4%)
  other arithmetic  1.1 us (1%)
    all_to_all x3, blocking collectives, exchanged(): return lax.all_to_all(x, axes, 0, 0, axis_index_groups=groups, tiled=True)  38.6 us
    all_to_all x1, starting transfers between devices, exchanged(): return lax.all_to_all(x, axes, 0, 0, axis_index_groups=groups, tiled=True)  31.8 us
    pallas_call x7, Pallas kernels, call(): pl.pallas_call(kernel, out_shape=outs, in_specs=[vmem] * len(args), out_s...  14.3 us
    ppermute x2, starting transfers between devices, shifted(): return lax.ppermute(block, axes, route)  4.78 us
    unnamed x17, local copies, waits for them, and re-layouts  3.98 us
  transfers between devices with their start and end apart: 3, of which 0 were waited for; matrix products, arithmetic and copies ran while one was open for 0% of the time, Pallas kernels for 7%

profile of v2, /device:TPU:2, one launch (start us, length us, event | category | flops | bytes accessed | tf_op | source)
XLA Modules:
  0.0 95.2 jit_solution(14135571969263640233)
XLA Ops:
  0.6 1.1 %multiply_convert_fusion.signal_ref = bf16[128,1024]{1,0:T(8,128)(2,1)S(1)} fusion(bf16[1,128,1024]{2,1,0:T(8,128)(2,1)} %param.8, bf16[1,128,1024]{2,1,0:T(8,128)(2,1)} %param.7), kind=kLoop, calls=%fused_computation | loop fusion | flops 524288 | bytes 786432 | tf_op jit(solution)/shard_map/convert_element_type | solution.py:221
  1.7 3.5 %collective-permute-start = (bf16[128,1024]{1,0:T(8,128)(2,1)S(1)}, bf16[128,1024]{1,0:T(8,128)(2,1)S(1)}, u32[]{:S(2)}, u32[]{:S(2)}) collective-permute-start(bf16[128,1024]{1,0:T(8,128)(2,1)S(1)} %multiply_convert_fusion.signal_ref), channel_id=1, source_target_pairs={{0,8},{8,16},{16,24},{24,32},{32,40},{40,48},{48,56},{56,64},{64,7... | collective-permute-start | bytes 786440 | tf_op jit(solution)/shard_map/ppermute | solution.py:23
  5.2 0.0 copy-start
  5.2 0.9 copy-done
  6.2 0.0 copy-start.1
  6.2 0.9 copy-done.1
  7.1 0.0 copy-start.4
  7.1 0.8 copy-done.4
  7.9 0.0 copy-start.6
  7.9 0.7 copy-done.6
  8.6 0.0 copy-start.7
  8.6 2.2 %shard_map.101 = (bf16[64,128,256]{2,1,0:T(8,128)(2,1)S(1)}, bf16[128,1024]{1,0:T(8,128)(2,1)S(1)}, bf16[128,1024]{1,0:T(8,128)(2,1)S(1)}, f32[128,1024]{1,0:T(8,128)S(1)}) custom-call(f32[64,128]{1,0:T(8,128)S(1)} %copy-done.4, bf16[128,1024]{1,0:T(8,128)(2,1)S(1)} %multiply_convert_fusion.signal_ref, bf16[128,1024]{1,0:T(8,128)(2,1)S(1)} %bitcast.12, ...), custom_call_target="tpu_custom_call" | custom-call | bytes 6066176 | tf_op jit(solution)/shard_map/pallas_call | solution.py:34
  10.8 0.0 collective-permute-done.before_ref
  10.8 0.0 copy-start.2
  10.8 0.0 copy-start.3
  10.8 0.0 copy-start.5
  10.8 2.5 %shard_map.102 = (f32[128,1024]{1,0:T(8,128)S(1)}, f32[8,2,128]{2,1,0:T(2,128)S(1)}) custom-call(bf16[64,128,256]{2,1,0:T(8,128)(2,1)S(1)} %get-tuple-element.25.weights_ref, bf16[128,1024]{1,0:T(8,128)(2,1)S(1)} %collective-permute-done.before_ref, bf16[128,1024]{1,0:T(8,128)(2,1)S(1)} %multiply_convert_fusion.signal_ref, ...), custom_call_target="tpu_custom_call" | custom-call | flops 536870912 | bytes 6037504 | tf_op jit(solution)/shard_map/pallas_call | solution.py:34
  13.3 17.2 %all_to_all.20.sums_ref = f32[8,2,128]{2,1,0:T(2,128)S(1)} all-to-all(f32[8,2,128]{2,1,0:T(2,128)S(1)} %get-tuple-element.28), channel_id=1, replica_groups=mesh['zh'=8,'zl'=4,'y'=4,'chan'=8] {'chan'}, dimensions={0} | all-to-all | bytes 16384 | tf_op jit(solution)/shard_map/all_to_all | solution.py:27
  30.5 4.3 %shard_map.103 = (bf16[128,1024]{1,0:T(8,128)(2,1)S(1)}, f32[16,4,128]{2,1,0:T(4,128)S(1)}) custom-call(f32[8,2,128]{2,1,0:T(2,128)S(1)} %all_to_all.20.sums_ref, f32[128,1024]{1,0:T(8,128)S(1)} %get-tuple-element.29.mixed_ref, bf16[128,1024]{1,0:T(8,128)(2,1)S(1)} %get-tuple-element.26.query_ref, f32[128,1024]{1,0:T(8,128)S(1)} %get-tuple-element.27.scaled_ref, ...), custom_call_target="tpu_custom_call" | custom-call | flops 536870912 | bytes 2138112 | tf_op jit(solution)/shard_map/pallas_call | solution.py:34
  34.8 10.7 %all_to_all.21.parts_ref = f32[16,4,128]{2,1,0:T(4,128)S(1)} all-to-all(f32[16,4,128]{2,1,0:T(4,128)S(1)} %get-tuple-element.31), channel_id=1, replica_groups=mesh['zh'=8,'zl'=4,'y'=4,'chan'=8] {'zl','y'}, dimensions={0} | all-to-all | bytes 65536 | tf_op jit(solution)/shard_map/all_to_all | solution.py:27
  45.5 0.6 shard_map.104
  46.1 1.3 %collective-permute-start.1 = (bf16[128,1024]{1,0:T(8,128)(2,1)S(1)}, bf16[128,1024]{1,0:T(8,128)(2,1)S(1)}, u32[]{:S(2)}, u32[]{:S(2)}) collective-permute-start(bf16[128,1024]{1,0:T(8,128)(2,1)S(1)} %get-tuple-element.37.conv_ref), channel_id=1, source_target_pairs={{8,0},{16,8},{24,16},{32,24},{40,32},{48,40},{56,48},{64,56},{72,6... | collective-permute-start | bytes 786440 | tf_op jit(solution)/shard_map/ppermute | solution.py:23
  47.4 31.8 %all-to-all-start.2 = ((f32[8,4,128]{2,1,0:T(4,128)}), f32[8,4,128]{2,1,0:T(4,128)S(1)}, u32[]{:S(2)}, u32[]{:S(2)}) async-start(f32[8,4,128]{2,1,0:T(4,128)} %shard_map.104), calls=%async_computation.2 | async-start | bytes 32768 | tf_op jit(solution)/shard_map/all_to_all | solution.py:27
  79.2 0.0 copy-done.7
  79.2 1.0 %shard_map.105 = (bf16[128,1024]{1,0:T(8,128)(2,1)}, bf16[128,1024]{1,0:T(8,128)(2,1)}) custom-call(f32[8,2,128]{2,1,0:T(2,128)S(1)} %all_to_all.20.sums_ref, f32[128,1024]{1,0:T(8,128)S(1)} %get-tuple-element.29.mixed_ref, bf16[128,1024]{1,0:T(8,128)(2,1)S(1)} %get-tuple-element.26.query_ref, f32[128,1024]{1,0:T(8,128)S(1)} %get-tuple-element.27.scaled_ref, ...), custom_call_target="tpu_custom_call" | custom-call | bytes 1847296 | tf_op jit(solution)/shard_map/pallas_call | solution.py:34
  80.2 0.0 collective-permute-done.1.after_ref
  80.3 0.0 copy-done.2
  80.3 0.0 copy-done.3
  80.3 0.0 copy-done.5
  80.3 3.6 %shard_map.106 = (bf16[128,1024]{1,0:T(8,128)(2,1)}, bf16[128,1024]{1,0:T(8,128)(2,1)}) custom-call(f32[64,128]{1,0:T(8,128)S(1)} %copy-done.5, bf16[128,1024]{1,0:T(8,128)(2,1)S(1)} %get-tuple-element.37.conv_ref, bf16[128,1024]{1,0:T(8,128)(2,1)S(1)} %collective-permute-done.1.after_ref, bf16[128,1024]{1,0:T(8,128)(2,1)S(1)} %bitcast.15, ...), custom_call_target="tpu_custom_call" | custom-call | flops 536870912 | bytes 1605632 | tf_op jit(solution)/shard_map/pallas_call | solution.py:34
  83.9 0.0 all-to-all-done.2.parts_ref
  83.9 10.7 %all_to_all.22 = f32[16,4,128]{2,1,0:T(4,128)S(1)} all-to-all(f32[16,4,128]{2,1,0:T(4,128)S(1)} %shard_map.107), channel_id=1, replica_groups=mesh['zh'=8,'zl'=4,'y'=4,'chan'=8] {'zl','y'}, dimensions={0} | all-to-all | bytes 65536 | tf_op jit(solution)/shard_map/all_to_all | solution.py:27
  94.6 0.6 copy.12
  (1 shorter events, 0.0 us)
Async XLA Ops:
  1.7 9.1 %collective-permute-start = (bf16[128,1024]{1,0:T(8,128)(2,1)S(1)}, bf16[128,1024]{1,0:T(8,128)(2,1)S(1)}, u32[]{:S(2)}, u32[]{:S(2)}) collective-permute-start(bf16[128,1024]{1,0:T(8,128)(2,1)S(1)} %multiply_convert_fusion.signal_ref), channel_id=1, source_target_pairs={{0,8},{8,16},{16,24},{24,32},{32,40},{40,48},{48,56},{56,64},{64,7... | collective-permute-start | bytes 786440 | tf_op jit(solution)/shard_map/ppermute | solution.py:23
  5.2 1.0 %copy-start = (bf16[1,128,1024]{2,1,0:T(8,128)(2,1)S(1)}, bf16[1,128,1024]{2,1,0:T(8,128)(2,1)}, u32[]{:S(2)}) copy-start(bf16[1,128,1024]{2,1,0:T(8,128)(2,1)} %param.6) | copy-start | bytes 786436
  6.2 0.9 copy-start.1
  7.1 0.8 copy-start.4
  7.9 0.7 copy-start.6
  8.6 70.6 %copy-start.7 = (f32[1024]{0:T(1024)S(1)}, f32[1024]{0:T(1024)}, u32[]{:S(2)}) copy-start(f32[1024]{0:T(1024)} %param.11) | copy-start | bytes 12292
  10.8 69.4 %copy-start.2 = (bf16[1,128,1024]{2,1,0:T(8,128)(2,1)S(1)}, bf16[1,128,1024]{2,1,0:T(8,128)(2,1)}, u32[]{:S(2)}) copy-start(bf16[1,128,1024]{2,1,0:T(8,128)(2,1)} %param.8) | copy-start | bytes 786436
  10.8 69.4 %copy-start.3 = (bf16[1,128,1024]{2,1,0:T(8,128)(2,1)S(1)}, bf16[1,128,1024]{2,1,0:T(8,128)(2,1)}, u32[]{:S(2)}) copy-start(bf16[1,128,1024]{2,1,0:T(8,128)(2,1)} %param.7) | copy-start | bytes 786436
  10.8 69.4 %copy-start.5 = (f32[64,128]{1,0:T(8,128)S(1)}, f32[64,128]{1,0:T(8,128)}, u32[]{:S(2)}) copy-start(f32[64,128]{1,0:T(8,128)} %filters_ref.3) | copy-start | bytes 98308
  46.1 34.1 %collective-permute-start.1 = (bf16[128,1024]{1,0:T(8,128)(2,1)S(1)}, bf16[128,1024]{1,0:T(8,128)(2,1)S(1)}, u32[]{:S(2)}, u32[]{:S(2)}) collective-permute-start(bf16[128,1024]{1,0:T(8,128)(2,1)S(1)} %get-tuple-element.37.conv_ref), channel_id=1, source_target_pairs={{8,0},{16,8},{24,16},{32,24},{40,32},{48,40},{56,48},{64,56},{72,6... | collective-permute-start | bytes 786440 | tf_op jit(solution)/shard_map/ppermute | solution.py:23
  47.4 36.5 %all-to-all-start.2 = ((f32[8,4,128]{2,1,0:T(4,128)}), f32[8,4,128]{2,1,0:T(4,128)S(1)}, u32[]{:S(2)}, u32[]{:S(2)}) async-start(f32[8,4,128]{2,1,0:T(4,128)} %shard_map.104), calls=%async_computation.2 | async-start | bytes 32768 | tf_op jit(solution)/shard_map/all_to_all | solution.py:27

commit v3 on v2

--- a/solution.py
+++ b/solution.py
@@ -241,22 +241,20 @@
         flops=conv_flops,
     )
     totals = exchanged(totals, NEAR)
-    (totals,) = call(gather_sum_kernel, [shaped((far, groups // near, taps), F32)], totals)
-    totals, conv, sums = lax.optimization_barrier((totals, conv, sums))
-    order = [(i + far // 2) % far for i in range(far)]
-    totals = exchanged(totals, FAR, [order])
     after = shifted(conv, CTX, -1)
     normed, grad_query = call(
         output_kernel, [block, block], sums, mixed, held, scaled, gain
     )
-    grad_key, grad_value = call(
-        back_kernel, [block, block], filters, conv, after, key_in, value_in, flops=conv_flops
-    )
-    totals, normed, grad_query, grad_key, grad_value = lax.optimization_barrier(
-        (totals, normed, grad_query, grad_key, grad_value)
-    )
+    totals, normed, grad_query = lax.optimization_barrier((totals, normed, grad_query))
+    (totals,) = call(gather_sum_kernel, [shaped((far, groups // near, taps), F32)], totals)
+    order = [(i + far // 2) % far for i in range(far)]
+    totals = exchanged(totals, FAR, [order])
     (totals,) = call(gather_sum_kernel, [shaped((near, groups // near, taps), F32)], totals)
     grad_filters = exchanged(totals, NEAR).reshape(groups, taps)
+    grad_key, grad_value = call(
+        back_kernel, [block, block], filters, conv, after, key_in, value_in,
+        flops=conv_flops,
+    )
     return tuple(a[None] for a in (normed, grad_query, grad_key, grad_value)) + (grad_filters,)
 
 

time: 95.7 us -> 93.6 us (0.978)
  blocking collectives: 38.6 us -> 17.2 us
  waiting for transfers between devices: 0.01 us -> 12.9 us
  starting transfers between devices: 36.6 us -> 41.6 us
  Pallas kernels: 14.3 us -> 15.5 us
    all_to_all x3 -> x1, blocking collectives: 38.6 us -> 17.2 us  [exchanged(): return lax.all_to_all(x, axes, 0, 0, axis_index_groups=groups, tiled=True)]
    all_to_all x1 -> x3, waiting for transfers between devices: 0.01 us -> 11.4 us  [exchanged(): return lax.all_to_all(x, axes, 0, 0, axis_index_groups=groups, tiled=True)]
    all_to_all x1 -> x3, starting transfers between devices: 31.8 us -> 36.8 us  [exchanged(): return lax.all_to_all(x, axes, 0, 0, axis_index_groups=groups, tiled=True)]
    ppermute x2, waiting for transfers between devices: 0.01 us -> 1.54 us  [shifted(): return lax.ppermute(block, axes, route)]
    pallas_call x7, Pallas kernels: 14.3 us -> 15.5 us  [call(): pl.pallas_call(kernel, out_shape=outs, in_specs=[vmem] * len(args), out_s...]
  transfers between devices with their start and end apart: 3 -> 5, of which waited for: 0 -> 4; matrix products, arithmetic and copies ran while one was open for 0% -> 0% of each run, Pallas kernels for 7% -> 8%
where the time goes in v3:
time: 93.6 us; the launch traced here: 93 us
  starting transfers between devices  41.6 us (44%)
  blocking collectives  17.2 us (18%)
  Pallas kernels  15.5 us (17%)
  waiting for transfers between devices  12.9 us (14%)
  local copies, waits for them, and re-layouts  3.98 us (4%)
  other arithmetic  1.1 us (1%)
    all_to_all x3, starting transfers between devices, exchanged(): return lax.all_to_all(x, axes, 0, 0, axis_index_groups=groups, tiled=True)  36.8 us
    all_to_all x1, blocking collectives, exchanged(): return lax.all_to_all(x, axes, 0, 0, axis_index_groups=groups, tiled=True)  17.2 us
    pallas_call x7, Pallas kernels, call(): pl.pallas_call(kernel, out_shape=outs, in_specs=[vmem] * len(args), out_s...  15.5 us
    all_to_all x3, waiting for transfers between devices, exchanged(): return lax.all_to_all(x, axes, 0, 0, axis_index_groups=groups, tiled=True)  11.4 us
    ppermute x2, starting transfers between devices, shifted(): return lax.ppermute(block, axes, route)  4.78 us
    unnamed x17, local copies, waits for them, and re-layouts  3.98 us
  transfers between devices with their start and end apart: 5, of which 4 were waited for; matrix products, arithmetic and copies ran while one was open for 0% of the time, Pallas kernels for 8%

profile of v3, /device:TPU:2, one launch (start us, length us, event | category | flops | bytes accessed | tf_op | source)
XLA Modules:
  0.0 93.0 jit_solution(14284527711733524317)
XLA Ops:
  0.6 1.1 %multiply_convert_fusion.signal_ref = bf16[128,1024]{1,0:T(8,128)(2,1)S(1)} fusion(bf16[1,128,1024]{2,1,0:T(8,128)(2,1)} %param.8, bf16[1,128,1024]{2,1,0:T(8,128)(2,1)} %param.7), kind=kLoop, calls=%fused_computation | loop fusion | flops 524288 | bytes 786432 | tf_op jit(solution)/shard_map/convert_element_type | solution.py:221
  1.7 3.5 %collective-permute-start = (bf16[128,1024]{1,0:T(8,128)(2,1)S(1)}, bf16[128,1024]{1,0:T(8,128)(2,1)S(1)}, u32[]{:S(2)}, u32[]{:S(2)}) collective-permute-start(bf16[128,1024]{1,0:T(8,128)(2,1)S(1)} %multiply_convert_fusion.signal_ref), channel_id=1, source_target_pairs={{0,8},{8,16},{16,24},{24,32},{32,40},{40,48},{48,56},{56,64},{64,7... | collective-permute-start | bytes 786440 | tf_op jit(solution)/shard_map/ppermute | solution.py:23
  5.2 0.0 copy-start
  5.2 0.9 %copy-done = bf16[1,128,1024]{2,1,0:T(8,128)(2,1)S(1)} copy-done((bf16[1,128,1024]{2,1,0:T(8,128)(2,1)S(1)}, bf16[1,128,1024]{2,1,0:T(8,128)(2,1)}, u32[]{:S(2)}) %copy-start) | copy-done | bytes 262168
  6.2 0.0 copy-start.1
  6.2 0.9 %copy-done.1 = bf16[1,128,1024]{2,1,0:T(8,128)(2,1)S(1)} copy-done((bf16[1,128,1024]{2,1,0:T(8,128)(2,1)S(1)}, bf16[1,128,1024]{2,1,0:T(8,128)(2,1)}, u32[]{:S(2)}) %copy-start.1) | copy-done | bytes 262168
  7.1 0.0 copy-start.4
  7.1 0.8 copy-done.4
  7.9 0.0 copy-start.6
  7.9 0.7 copy-done.6
  8.6 0.0 copy-start.7
  8.6 2.2 %shard_map.101 = (bf16[64,128,256]{2,1,0:T(8,128)(2,1)S(1)}, bf16[128,1024]{1,0:T(8,128)(2,1)S(1)}, bf16[128,1024]{1,0:T(8,128)(2,1)S(1)}, f32[128,1024]{1,0:T(8,128)S(1)}) custom-call(f32[64,128]{1,0:T(8,128)S(1)} %copy-done.4, bf16[128,1024]{1,0:T(8,128)(2,1)S(1)} %multiply_convert_fusion.signal_ref, bf16[128,1024]{1,0:T(8,128)(2,1)S(1)} %bitcast.12, ...), custom_call_target="tpu_custom_call" | custom-call | bytes 6066176 | tf_op jit(solution)/shard_map/pallas_call | solution.py:34
  10.8 0.0 collective-permute-done.before_ref
  10.8 0.0 copy-start.2
  10.8 0.0 copy-start.3
  10.8 0.0 copy-start.5
  10.8 2.5 %shard_map.102 = (f32[128,1024]{1,0:T(8,128)S(1)}, f32[8,2,128]{2,1,0:T(2,128)S(1)}) custom-call(bf16[64,128,256]{2,1,0:T(8,128)(2,1)S(1)} %get-tuple-element.20.weights_ref, bf16[128,1024]{1,0:T(8,128)(2,1)S(1)} %collective-permute-done.before_ref, bf16[128,1024]{1,0:T(8,128)(2,1)S(1)} %multiply_convert_fusion.signal_ref, ...), custom_call_target="tpu_custom_call" | custom-call | flops 536870912 | bytes 6037504 | tf_op jit(solution)/shard_map/pallas_call | solution.py:34
  13.3 17.2 %all_to_all.20.sums_ref = f32[8,2,128]{2,1,0:T(2,128)S(1)} all-to-all(f32[8,2,128]{2,1,0:T(2,128)S(1)} %get-tuple-element.23), channel_id=1, replica_groups=mesh['zh'=8,'zl'=4,'y'=4,'chan'=8] {'chan'}, dimensions={0} | all-to-all | bytes 16384 | tf_op jit(solution)/shard_map/all_to_all | solution.py:27
  30.5 4.9 %shard_map.103 = (bf16[128,1024]{1,0:T(8,128)(2,1)S(1)}, f32[16,4,128]{2,1,0:T(4,128)}) custom-call(f32[8,2,128]{2,1,0:T(2,128)S(1)} %all_to_all.20.sums_ref, f32[128,1024]{1,0:T(8,128)S(1)} %get-tuple-element.24.mixed_ref, bf16[128,1024]{1,0:T(8,128)(2,1)S(1)} %get-tuple-element.21.query_ref, f32[128,1024]{1,0:T(8,128)S(1)} %get-tuple-element.22.scaled_ref, ...), custom_call_target="tpu_custom_call" | custom-call | flops 536870912 | bytes 2138112 | tf_op jit(solution)/shard_map/pallas_call | solution.py:34
  35.4 3.5 %all-to-all-start.1 = ((f32[16,4,128]{2,1,0:T(4,128)}), f32[16,4,128]{2,1,0:T(4,128)S(1)}, u32[]{:S(2)}, u32[]{:S(2)}) async-start(f32[16,4,128]{2,1,0:T(4,128)} %get-tuple-element.26), calls=%async_computation.1 | async-start | bytes 65536 | tf_op jit(solution)/shard_map/all_to_all | solution.py:27
  38.9 0.0 copy-done.7
  38.9 1.0 %shard_map.104 = (bf16[128,1024]{1,0:T(8,128)(2,1)}, bf16[128,1024]{1,0:T(8,128)(2,1)}) custom-call(f32[8,2,128]{2,1,0:T(2,128)S(1)} %all_to_all.20.sums_ref, f32[128,1024]{1,0:T(8,128)S(1)} %get-tuple-element.24.mixed_ref, bf16[128,1024]{1,0:T(8,128)(2,1)S(1)} %get-tuple-element.21.query_ref, f32[128,1024]{1,0:T(8,128)S(1)} %get-tuple-element.22.scaled_ref, ...), custom_call_target="tpu_custom_call" | custom-call | bytes 1847296 | tf_op jit(solution)/shard_map/pallas_call | solution.py:34
  40.0 7.1 %all-to-all-done.1.parts_ref = f32[16,4,128]{2,1,0:T(4,128)S(1)} async-done(((f32[16,4,128]{2,1,0:T(4,128)}), f32[16,4,128]{2,1,0:T(4,128)S(1)}, u32[]{:S(2)}, u32[]{:S(2)}) %all-to-all-start.1) | async-done | bytes 32800 | tf_op jit(solution)/shard_map/all_to_all | solution.py:27
  47.0 0.6 shard_map.106
  47.7 29.8 %all-to-all-start.2 = ((f32[8,4,128]{2,1,0:T(4,128)}), f32[8,4,128]{2,1,0:T(4,128)S(1)}, u32[]{:S(2)}, u32[]{:S(2)}) async-start(f32[8,4,128]{2,1,0:T(4,128)} %shard_map.106), calls=%async_computation.2 | async-start | bytes 32768 | tf_op jit(solution)/shard_map/all_to_all | solution.py:27
  77.5 1.3 %collective-permute-start.1 = (bf16[128,1024]{1,0:T(8,128)(2,1)S(1)}, bf16[128,1024]{1,0:T(8,128)(2,1)S(1)}, u32[]{:S(2)}, u32[]{:S(2)}) collective-permute-start(bf16[128,1024]{1,0:T(8,128)(2,1)S(1)} %get-tuple-element.31.conv_ref), channel_id=1, source_target_pairs={{8,0},{16,8},{24,16},{32,24},{40,32},{48,40},{56,48},{64,56},{72,6... | collective-permute-start | bytes 786440 | tf_op jit(solution)/shard_map/ppermute | solution.py:23
  78.8 1.4 %all-to-all-done.2.parts_ref = f32[8,4,128]{2,1,0:T(4,128)S(1)} async-done(((f32[8,4,128]{2,1,0:T(4,128)}), f32[8,4,128]{2,1,0:T(4,128)S(1)}, u32[]{:S(2)}, u32[]{:S(2)}) %all-to-all-start.2) | async-done | bytes 16416 | tf_op jit(solution)/shard_map/all_to_all | solution.py:27
  80.2 0.6 shard_map.107
  80.8 3.5 %all-to-all-start.3 = ((f32[16,4,128]{2,1,0:T(4,128)}), f32[16,4,128]{2,1,0:T(4,128)S(1)}, u32[]{:S(2)}, u32[]{:S(2)}) async-start(f32[16,4,128]{2,1,0:T(4,128)} %shard_map.107), calls=%async_computation.3 | async-start | bytes 65536 | tf_op jit(solution)/shard_map/all_to_all | solution.py:27
  84.3 1.5 %collective-permute-done.1.after_ref = bf16[128,1024]{1,0:T(8,128)(2,1)S(1)} collective-permute-done((bf16[128,1024]{1,0:T(8,128)(2,1)S(1)}, bf16[128,1024]{1,0:T(8,128)(2,1)S(1)}, u32[]{:S(2)}, u32[]{:S(2)}) %collective-permute-start.1) | collective-permute-done | bytes 262176 | tf_op jit(solution)/shard_map/ppermute | solution.py:23
  85.9 0.0 copy-done.2
  85.9 0.0 copy-done.3
  85.9 0.0 copy-done.5
  85.9 3.6 %shard_map.105 = (bf16[128,1024]{1,0:T(8,128)(2,1)}, bf16[128,1024]{1,0:T(8,128)(2,1)}) custom-call(f32[64,128]{1,0:T(8,128)S(1)} %copy-done.5, bf16[128,1024]{1,0:T(8,128)(2,1)S(1)} %get-tuple-element.31.conv_ref, bf16[128,1024]{1,0:T(8,128)(2,1)S(1)} %collective-permute-done.1.after_ref, bf16[128,1024]{1,0:T(8,128)(2,1)S(1)} %bitcast.15, ...), custom_call_target="tpu_custom_call" | custom-call | flops 536870912 | bytes 1605632 | tf_op jit(solution)/shard_map/pallas_call | solution.py:34
  89.5 2.9 %all-to-all-done.3 = f32[16,4,128]{2,1,0:T(4,128)S(1)} async-done(((f32[16,4,128]{2,1,0:T(4,128)}), f32[16,4,128]{2,1,0:T(4,128)S(1)}, u32[]{:S(2)}, u32[]{:S(2)}) %all-to-all-start.3) | async-done | bytes 32800 | tf_op jit(solution)/shard_map/all_to_all | solution.py:27
  92.4 0.6 copy.12
Async XLA Ops:
  1.7 9.1 %collective-permute-start = (bf16[128,1024]{1,0:T(8,128)(2,1)S(1)}, bf16[128,1024]{1,0:T(8,128)(2,1)S(1)}, u32[]{:S(2)}, u32[]{:S(2)}) collective-permute-start(bf16[128,1024]{1,0:T(8,128)(2,1)S(1)} %multiply_convert_fusion.signal_ref), channel_id=1, source_target_pairs={{0,8},{8,16},{16,24},{24,32},{32,40},{40,48},{48,56},{56,64},{64,7... | collective-permute-start | bytes 786440 | tf_op jit(solution)/shard_map/ppermute | solution.py:23
  5.2 1.0 %copy-start = (bf16[1,128,1024]{2,1,0:T(8,128)(2,1)S(1)}, bf16[1,128,1024]{2,1,0:T(8,128)(2,1)}, u32[]{:S(2)}) copy-start(bf16[1,128,1024]{2,1,0:T(8,128)(2,1)} %param.6) | copy-start | bytes 786436
  6.2 0.9 %copy-start.1 = (bf16[1,128,1024]{2,1,0:T(8,128)(2,1)S(1)}, bf16[1,128,1024]{2,1,0:T(8,128)(2,1)}, u32[]{:S(2)}) copy-start(bf16[1,128,1024]{2,1,0:T(8,128)(2,1)} %param.9) | copy-start | bytes 786436
  7.1 0.8 copy-start.4
  7.9 0.7 copy-start.6
  8.6 30.3 %copy-start.7 = (f32[1024]{0:T(1024)S(1)}, f32[1024]{0:T(1024)}, u32[]{:S(2)}) copy-start(f32[1024]{0:T(1024)} %param.11) | copy-start | bytes 12292
  10.8 75.0 %copy-start.2 = (bf16[1,128,1024]{2,1,0:T(8,128)(2,1)S(1)}, bf16[1,128,1024]{2,1,0:T(8,128)(2,1)}, u32[]{:S(2)}) copy-start(bf16[1,128,1024]{2,1,0:T(8,128)(2,1)} %param.8) | copy-start | bytes 786436
  10.8 75.0 %copy-start.3 = (bf16[1,128,1024]{2,1,0:T(8,128)(2,1)S(1)}, bf16[1,128,1024]{2,1,0:T(8,128)(2,1)}, u32[]{:S(2)}) copy-start(bf16[1,128,1024]{2,1,0:T(8,128)(2,1)} %param.7) | copy-start | bytes 786436
  10.8 75.0 %copy-start.5 = (f32[64,128]{1,0:T(8,128)S(1)}, f32[64,128]{1,0:T(8,128)}, u32[]{:S(2)}) copy-start(f32[64,128]{1,0:T(8,128)} %filters_ref.3) | copy-start | bytes 98308
  35.4 11.6 %all-to-all-start.1 = ((f32[16,4,128]{2,1,0:T(4,128)}), f32[16,4,128]{2,1,0:T(4,128)S(1)}, u32[]{:S(2)}, u32[]{:S(2)}) async-start(f32[16,4,128]{2,1,0:T(4,128)} %get-tuple-element.26), calls=%async_computation.1 | async-start | bytes 65536 | tf_op jit(solution)/shard_map/all_to_all | solution.py:27
  47.7 32.5 %all-to-all-start.2 = ((f32[8,4,128]{2,1,0:T(4,128)}), f32[8,4,128]{2,1,0:T(4,128)S(1)}, u32[]{:S(2)}, u32[]{:S(2)}) async-start(f32[8,4,128]{2,1,0:T(4,128)} %shard_map.106), calls=%async_computation.2 | async-start | bytes 32768 | tf_op jit(solution)/shard_map/all_to_all | solution.py:27
  77.5 8.4 %collective-permute-start.1 = (bf16[128,1024]{1,0:T(8,128)(2,1)S(1)}, bf16[128,1024]{1,0:T(8,128)(2,1)S(1)}, u32[]{:S(2)}, u32[]{:S(2)}) collective-permute-start(bf16[128,1024]{1,0:T(8,128)(2,1)S(1)} %get-tuple-element.31.conv_ref), channel_id=1, source_target_pairs={{8,0},{16,8},{24,16},{32,24},{40,32},{48,40},{56,48},{64,56},{72,6... | collective-permute-start | bytes 786440 | tf_op jit(solution)/shard_map/ppermute | solution.py:23
  80.8 11.6 %all-to-all-start.3 = ((f32[16,4,128]{2,1,0:T(4,128)}), f32[16,4,128]{2,1,0:T(4,128)S(1)}, u32[]{:S(2)}, u32[]{:S(2)}) async-start(f32[16,4,128]{2,1,0:T(4,128)} %shard_map.107), calls=%async_computation.3 | async-start | bytes 65536 | tf_op jit(solution)/shard_map/all_to_all | solution.py:27

commit v4 on v3

--- a/solution.py
+++ b/solution.py
@@ -1,3 +1,5 @@
+import math
+
 import jax
 import jax.numpy as jnp
 from jax import lax
@@ -27,14 +29,19 @@
     return lax.all_to_all(x, axes, 0, 0, axis_index_groups=groups, tiled=True)
 
 
-def call(kernel, outs, *args, flops=0, scratch=()):
+def call(kernel, outs, *args, flops=0, scratch=(), outside=()):
     moved = sum(a.size * a.dtype.itemsize for a in args)
-    moved += sum(o.size * o.dtype.itemsize for o in outs)
+    moved += sum(math.prod(o.shape) * o.dtype.itemsize for o in outs)
     vmem = pl.BlockSpec(memory_space=pltpu.VMEM)
+    hbm = pl.BlockSpec(memory_space=pltpu.HBM)
+    args = [
+        pltpu.with_memory_space_constraint(a, pltpu.HBM) if i in outside else a
+        for i, a in enumerate(args)
+    ]
     return pl.pallas_call(
         kernel,
         out_shape=outs,
-        in_specs=[vmem] * len(args),
+        in_specs=[hbm if i in outside else vmem for i in range(len(args))],
         out_specs=[vmem] * len(outs),
         scratch_shapes=scratch,
         compiler_params=pltpu.CompilerParams(vmem_limit_bytes=VMEM_LIMIT),
@@ -61,14 +68,25 @@
 
 def prepare_kernel(
     filters_ref, signal_ref, query_ref, cot_ref, gain_ref,
-    weights_ref, mirror_ref, held_ref, scaled_ref, back_taps_ref,
+    weights_ref, mirror_ref, held_ref, scaled_ref, taps_ref, back_taps_ref, cot_copy, gain_copy, sems,
 ):
     groups, taps = filters_ref.shape
+    copies = [
+        pltpu.make_async_copy(source, target, sems.at[i])
+        for i, (source, target) in enumerate(
+            [(filters_ref, taps_ref), (gain_ref, gain_copy), (cot_ref, cot_copy), (query_ref, held_ref)]
+        )
+    ]
+    for copy in copies:
+        copy.start()
     row, col = index((taps, taps), 0), index((taps, taps), 1)
+    swap = (row + col == taps - 1).astype(BF16)
+    mirror_ref[...] = jnp.dot(swap, signal_ref[...], preferred_element_type=F32).astype(BF16)
+    copies[0].wait()
     own = row >= col
     turn = (lax.rem(row + col, taps) == 0).astype(BF16)
     back_taps_ref[...] = jnp.dot(
-        filters_ref[...].astype(BF16), turn, preferred_element_type=F32
+        taps_ref[...].astype(BF16), turn, preferred_element_type=F32
     )
 
     def step(g, _):
@@ -78,10 +96,9 @@
         return 0
 
     lax.fori_loop(0, groups, step, 0, unroll=4)
-    swap = (row + col == taps - 1).astype(BF16)
-    mirror_ref[...] = jnp.dot(swap, signal_ref[...], preferred_element_type=F32).astype(BF16)
-    held_ref[...] = query_ref[...]
-    scaled_ref[...] = gain_ref[...] * cot_ref[...].astype(F32)
+    for copy in copies[1:]:
+        copy.wait()
+    scaled_ref[...] = gain_copy[...] * cot_copy[...].astype(F32)
 
 
 def mix_kernel(weights_ref, before_ref, signal_ref, query_ref, scaled_ref, mixed_ref, sums_ref):
@@ -225,7 +242,14 @@
         prepare_kernel,
         [shaped((groups, taps, 2 * taps), BF16), block, block, wide],
         filters, signal, query, cotangent, gain,
-        scratch=[pltpu.VMEM((groups, taps), F32)],
+        scratch=[
+            pltpu.VMEM((groups, taps), F32),
+            pltpu.VMEM((groups, taps), F32),
+            pltpu.VMEM((taps, width), BF16),
+            pltpu.VMEM((1, width), F32),
+            pltpu.SemaphoreType.DMA((4,)),
+        ],
+        outside=(0, 2, 3, 4),
     )
     mixed, sums = call(
         mix_kernel,
@@ -241,16 +265,16 @@
         flops=conv_flops,
     )
     totals = exchanged(totals, NEAR)
-    after = shifted(conv, CTX, -1)
-    normed, grad_query = call(
-        output_kernel, [block, block], sums, mixed, held, scaled, gain
-    )
-    totals, normed, grad_query = lax.optimization_barrier((totals, normed, grad_query))
     (totals,) = call(gather_sum_kernel, [shaped((far, groups // near, taps), F32)], totals)
     order = [(i + far // 2) % far for i in range(far)]
     totals = exchanged(totals, FAR, [order])
+    after = shifted(conv, CTX, -1)
     (totals,) = call(gather_sum_kernel, [shaped((near, groups // near, taps), F32)], totals)
     grad_filters = exchanged(totals, NEAR).reshape(groups, taps)
+    normed, grad_query = call(
+        output_kernel, [block, block], sums, mixed, held, scaled, gain
+    )
+    after, normed, grad_query = lax.optimization_barrier((after, normed, grad_query))
     grad_key, grad_value = call(
         back_kernel, [block, block], filters, conv, after, key_in, value_in,
         flops=conv_flops,

time: 93.6 us -> 91.9 us (0.982)
  blocking collectives: 17.2 us -> 27.3 us
  waiting for transfers between devices: 12.9 us -> 7.55 us
  local copies, waits for them, and re-layouts: 3.98 us -> 0.63 us
  starting transfers between devices: 41.6 us -> 38.7 us
    all_to_all x1 -> x2, blocking collectives: 17.2 us -> 27.3 us  [exchanged(): return lax.all_to_all(x, axes, 0, 0, axis_index_groups=groups, tiled=True)]
    all_to_all x3 -> x2, waiting for transfers between devices: 11.4 us -> 4.37 us  [exchanged(): return lax.all_to_all(x, axes, 0, 0, axis_index_groups=groups, tiled=True)]
    unnamed x17 -> x9, local copies, waits for them, and re-layouts: 3.98 us -> 0.63 us
    all_to_all x3 -> x2, starting transfers between devices: 36.8 us -> 34 us  [exchanged(): return lax.all_to_all(x, axes, 0, 0, axis_index_groups=groups, tiled=True)]
    ppermute x2, waiting for transfers between devices: 1.54 us -> 3.18 us  [shifted(): return lax.ppermute(block, axes, route)]
  transfers between devices with their start and end apart: 5 -> 4, of which waited for: 4 -> 4; matrix products, arithmetic and copies ran while one was open for 0% -> 0% of each run, Pallas kernels for 8% -> 9%
where the time goes in v4:
time: 91.9 us; the launch traced here: 91.5 us
  starting transfers between devices  38.7 us (42%)
  blocking collectives  27.3 us (30%)
  Pallas kernels  15.5 us (17%)
  waiting for transfers between devices  7.55 us (8%)
  other arithmetic  1.1 us (1%)
    all_to_all x2, starting transfers between devices, exchanged(): return lax.all_to_all(x, axes, 0, 0, axis_index_groups=groups, tiled=True)  34 us
    all_to_all x2, blocking collectives, exchanged(): return lax.all_to_all(x, axes, 0, 0, axis_index_groups=groups, tiled=True)  27.3 us
    pallas_call x7, Pallas kernels, call(): pl.pallas_call(kernel, out_shape=outs, in_specs=[hbm if i in outside else...  15.5 us
    ppermute x2, starting transfers between devices, shifted(): return lax.ppermute(block, axes, route)  4.78 us
    all_to_all x2, waiting for transfers between devices, exchanged(): return lax.all_to_all(x, axes, 0, 0, axis_index_groups=groups, tiled=True)  4.37 us
    ppermute x2, waiting for transfers between devices, shifted(): return lax.ppermute(block, axes, route)  3.18 us
  transfers between devices with their start and end apart: 4, of which 4 were waited for; matrix products, arithmetic and copies ran while one was open for 0% of the time, Pallas kernels for 9%

profile of v4, /device:TPU:2, one launch (start us, length us, event | category | flops | bytes accessed | tf_op | source)
XLA Modules:
  0.0 91.5 jit_solution(4250147537514381526)
XLA Ops:
  0.6 1.1 %multiply_convert_fusion.signal_ref = bf16[128,1024]{1,0:T(8,128)(2,1)S(1)} fusion(bf16[1,128,1024]{2,1,0:T(8,128)(2,1)} %param.8, bf16[1,128,1024]{2,1,0:T(8,128)(2,1)} %param.7), kind=kLoop, calls=%fused_computation | loop fusion | flops 524288 | bytes 786432 | tf_op jit(solution)/shard_map/convert_element_type | solution.py:238
  1.7 3.5 %collective-permute-start = (bf16[128,1024]{1,0:T(8,128)(2,1)S(1)}, bf16[128,1024]{1,0:T(8,128)(2,1)S(1)}, u32[]{:S(2)}, u32[]{:S(2)}) collective-permute-start(bf16[128,1024]{1,0:T(8,128)(2,1)S(1)} %multiply_convert_fusion.signal_ref), channel_id=1, source_target_pairs={{0,8},{8,16},{16,24},{24,32},{32,40},{40,48},{48,56},{56,64},{64,7... | collective-permute-start | bytes 786440 | tf_op jit(solution)/shard_map/ppermute | solution.py:25
  5.2 0.0 copy-start.3
  5.2 2.8 %shard_map.101 = (bf16[64,128,256]{2,1,0:T(8,128)(2,1)S(1)}, bf16[128,1024]{1,0:T(8,128)(2,1)S(1)}, bf16[128,1024]{1,0:T(8,128)(2,1)S(1)}, f32[128,1024]{1,0:T(8,128)S(1)}) custom-call(f32[64,128]{1,0:T(8,128)} %filters_ref.3, bf16[128,1024]{1,0:T(8,128)(2,1)S(1)} %multiply_convert_fusion.signal_ref, bf16[128,1024]{1,0:T(8,128)(2,1)} %bitcast.16, ...), custom_call_target="tpu_custom_call" | custom-call | bytes 6066176 | tf_op jit(solution)/shard_map/pallas_call | solution.py:41
  8.1 2.7 %collective-permute-done.before_ref = bf16[128,1024]{1,0:T(8,128)(2,1)S(1)} collective-permute-done((bf16[128,1024]{1,0:T(8,128)(2,1)S(1)}, bf16[128,1024]{1,0:T(8,128)(2,1)S(1)}, u32[]{:S(2)}, u32[]{:S(2)}) %collective-permute-start) | collective-permute-done | bytes 262176 | tf_op jit(solution)/shard_map/ppermute | solution.py:25
  10.8 0.0 copy-start
  10.8 0.0 copy-start.1
  10.8 0.0 copy-start.2
  10.8 2.5 %shard_map.102 = (f32[128,1024]{1,0:T(8,128)S(1)}, f32[8,2,128]{2,1,0:T(2,128)S(1)}) custom-call(bf16[64,128,256]{2,1,0:T(8,128)(2,1)S(1)} %get-tuple-element.20.weights_ref, bf16[128,1024]{1,0:T(8,128)(2,1)S(1)} %collective-permute-done.before_ref, bf16[128,1024]{1,0:T(8,128)(2,1)S(1)} %multiply_convert_fusion.signal_ref, ...), custom_call_target="tpu_custom_call" | custom-call | flops 536870912 | bytes 6037504 | tf_op jit(solution)/shard_map/pallas_call | solution.py:41
  13.2 15.5 %all_to_all.20.sums_ref = f32[8,2,128]{2,1,0:T(2,128)S(1)} all-to-all(f32[8,2,128]{2,1,0:T(2,128)S(1)} %get-tuple-element.23), channel_id=1, replica_groups=mesh['zh'=8,'zl'=4,'y'=4,'chan'=8] {'chan'}, dimensions={0} | all-to-all | bytes 16384 | tf_op jit(solution)/shard_map/all_to_all | solution.py:29
  28.8 4.3 %shard_map.103 = (bf16[128,1024]{1,0:T(8,128)(2,1)S(1)}, f32[16,4,128]{2,1,0:T(4,128)S(1)}) custom-call(f32[8,2,128]{2,1,0:T(2,128)S(1)} %all_to_all.20.sums_ref, f32[128,1024]{1,0:T(8,128)S(1)} %get-tuple-element.24.mixed_ref, bf16[128,1024]{1,0:T(8,128)(2,1)S(1)} %get-tuple-element.21.query_ref, f32[128,1024]{1,0:T(8,128)S(1)} %get-tuple-element.22.scaled_ref, ...), custom_call_target="tpu_custom_call" | custom-call | flops 536870912 | bytes 2138112 | tf_op jit(solution)/shard_map/pallas_call | solution.py:41
  33.1 11.8 %all_to_all.21.parts_ref = f32[16,4,128]{2,1,0:T(4,128)S(1)} all-to-all(f32[16,4,128]{2,1,0:T(4,128)S(1)} %get-tuple-element.34), channel_id=1, replica_groups=mesh['zh'=8,'zl'=4,'y'=4,'chan'=8] {'zl','y'}, dimensions={0} | all-to-all | bytes 65536 | tf_op jit(solution)/shard_map/all_to_all | solution.py:29
  44.9 0.6 shard_map.106
  45.5 30.5 %all-to-all-start.2 = ((f32[8,4,128]{2,1,0:T(4,128)}), f32[8,4,128]{2,1,0:T(4,128)S(1)}, u32[]{:S(2)}, u32[]{:S(2)}) async-start(f32[8,4,128]{2,1,0:T(4,128)} %shard_map.106), calls=%async_computation.2 | async-start | bytes 32768 | tf_op jit(solution)/shard_map/all_to_all | solution.py:29
  76.0 1.3 %collective-permute-start.1 = (bf16[128,1024]{1,0:T(8,128)(2,1)S(1)}, bf16[128,1024]{1,0:T(8,128)(2,1)S(1)}, u32[]{:S(2)}, u32[]{:S(2)}) collective-permute-start(bf16[128,1024]{1,0:T(8,128)(2,1)S(1)} %get-tuple-element.26.conv_ref), channel_id=1, source_target_pairs={{8,0},{16,8},{24,16},{32,24},{40,32},{48,40},{56,48},{64,56},{72,6... | collective-permute-start | bytes 786440 | tf_op jit(solution)/shard_map/ppermute | solution.py:25
  77.2 1.4 %all-to-all-done.2.parts_ref = f32[8,4,128]{2,1,0:T(4,128)S(1)} async-done(((f32[8,4,128]{2,1,0:T(4,128)}), f32[8,4,128]{2,1,0:T(4,128)S(1)}, u32[]{:S(2)}, u32[]{:S(2)}) %all-to-all-start.2) | async-done | bytes 16416 | tf_op jit(solution)/shard_map/all_to_all | solution.py:29
  78.7 0.6 shard_map.107
  79.3 3.5 %all-to-all-start.3 = ((f32[16,4,128]{2,1,0:T(4,128)}), f32[16,4,128]{2,1,0:T(4,128)S(1)}, u32[]{:S(2)}, u32[]{:S(2)}) async-start(f32[16,4,128]{2,1,0:T(4,128)} %shard_map.107), calls=%async_computation.3 | async-start | bytes 65536 | tf_op jit(solution)/shard_map/all_to_all | solution.py:29
  82.8 0.0 copy-done.3
  82.8 1.0 %shard_map.104 = (bf16[128,1024]{1,0:T(8,128)(2,1)}, bf16[128,1024]{1,0:T(8,128)(2,1)}) custom-call(f32[8,2,128]{2,1,0:T(2,128)S(1)} %all_to_all.20.sums_ref, f32[128,1024]{1,0:T(8,128)S(1)} %get-tuple-element.24.mixed_ref, bf16[128,1024]{1,0:T(8,128)(2,1)S(1)} %get-tuple-element.21.query_ref, f32[128,1024]{1,0:T(8,128)S(1)} %get-tuple-element.22.scaled_ref, ...), custom_call_target="tpu_custom_call" | custom-call | bytes 1847296 | tf_op jit(solution)/shard_map/pallas_call | solution.py:41
  83.8 0.5 collective-permute-done.1.after_ref
  84.3 0.0 copy-done
  84.3 0.0 copy-done.1
  84.3 0.0 copy-done.2
  84.4 3.6 %shard_map.105 = (bf16[128,1024]{1,0:T(8,128)(2,1)}, bf16[128,1024]{1,0:T(8,128)(2,1)}) custom-call(f32[64,128]{1,0:T(8,128)S(1)} %copy-done.2, bf16[128,1024]{1,0:T(8,128)(2,1)S(1)} %get-tuple-element.26.conv_ref, bf16[128,1024]{1,0:T(8,128)(2,1)S(1)} %collective-permute-done.1.after_ref, bf16[128,1024]{1,0:T(8,128)(2,1)S(1)} %bitcast.13, ...), custom_call_target="tpu_custom_call" | custom-call | flops 536870912 | bytes 1605632 | tf_op jit(solution)/shard_map/pallas_call | solution.py:41
  88.0 2.9 %all-to-all-done.3 = f32[16,4,128]{2,1,0:T(4,128)S(1)} async-done(((f32[16,4,128]{2,1,0:T(4,128)}), f32[16,4,128]{2,1,0:T(4,128)S(1)}, u32[]{:S(2)}, u32[]{:S(2)}) %all-to-all-start.3) | async-done | bytes 32800 | tf_op jit(solution)/shard_map/all_to_all | solution.py:29
  90.9 0.6 copy.12
Async XLA Ops:
  1.7 9.0 %collective-permute-start = (bf16[128,1024]{1,0:T(8,128)(2,1)S(1)}, bf16[128,1024]{1,0:T(8,128)(2,1)S(1)}, u32[]{:S(2)}, u32[]{:S(2)}) collective-permute-start(bf16[128,1024]{1,0:T(8,128)(2,1)S(1)} %multiply_convert_fusion.signal_ref), channel_id=1, source_target_pairs={{0,8},{8,16},{16,24},{24,32},{32,40},{40,48},{48,56},{56,64},{64,7... | collective-permute-start | bytes 786440 | tf_op jit(solution)/shard_map/ppermute | solution.py:25
  5.2 77.6 %copy-start.3 = (f32[1024]{0:T(1024)S(1)}, f32[1024]{0:T(1024)}, u32[]{:S(2)}) copy-start(f32[1024]{0:T(1024)} %param.11) | copy-start | bytes 12292
  10.8 73.6 %copy-start = (bf16[1,128,1024]{2,1,0:T(8,128)(2,1)S(1)}, bf16[1,128,1024]{2,1,0:T(8,128)(2,1)}, u32[]{:S(2)}) copy-start(bf16[1,128,1024]{2,1,0:T(8,128)(2,1)} %param.8) | copy-start | bytes 786436
  10.8 73.6 %copy-start.1 = (bf16[1,128,1024]{2,1,0:T(8,128)(2,1)S(1)}, bf16[1,128,1024]{2,1,0:T(8,128)(2,1)}, u32[]{:S(2)}) copy-start(bf16[1,128,1024]{2,1,0:T(8,128)(2,1)} %param.7) | copy-start | bytes 786436
  10.8 73.6 %copy-start.2 = (f32[64,128]{1,0:T(8,128)S(1)}, f32[64,128]{1,0:T(8,128)}, u32[]{:S(2)}) copy-start(f32[64,128]{1,0:T(8,128)} %filters_ref.3) | copy-start | bytes 98308
  45.5 33.2 %all-to-all-start.2 = ((f32[8,4,128]{2,1,0:T(4,128)}), f32[8,4,128]{2,1,0:T(4,128)S(1)}, u32[]{:S(2)}, u32[]{:S(2)}) async-start(f32[8,4,128]{2,1,0:T(4,128)} %shard_map.106), calls=%async_computation.2 | async-start | bytes 32768 | tf_op jit(solution)/shard_map/all_to_all | solution.py:29
  76.0 8.4 %collective-permute-start.1 = (bf16[128,1024]{1,0:T(8,128)(2,1)S(1)}, bf16[128,1024]{1,0:T(8,128)(2,1)S(1)}, u32[]{:S(2)}, u32[]{:S(2)}) collective-permute-start(bf16[128,1024]{1,0:T(8,128)(2,1)S(1)} %get-tuple-element.26.conv_ref), channel_id=1, source_target_pairs={{8,0},{16,8},{24,16},{32,24},{40,32},{48,40},{56,48},{64,56},{72,6... | collective-permute-start | bytes 786440 | tf_op jit(solution)/shard_map/ppermute | solution.py:25
  79.3 11.6 %all-to-all-start.3 = ((f32[16,4,128]{2,1,0:T(4,128)}), f32[16,4,128]{2,1,0:T(4,128)S(1)}, u32[]{:S(2)}, u32[]{:S(2)}) async-start(f32[16,4,128]{2,1,0:T(4,128)} %shard_map.107), calls=%async_computation.3 | async-start | bytes 65536 | tf_op jit(solution)/shard_map/all_to_all | solution.py:29

commit v5 on v4

--- a/solution.py
+++ b/solution.py
@@ -10,9 +10,7 @@
 
 
 D = 8192
-CTX = ("zh", "zl", "y")
-NEAR = ("zl", "y")
-FAR = "zh"
+CTX = ("far", "near")
 LANES = 128
 VMEM_LIMIT = 16 * 2**20
 F32 = jnp.float32
@@ -25,8 +23,10 @@
     return lax.ppermute(block, axes, route)
 
 
-def exchanged(x, axes, groups=None):
-    return lax.all_to_all(x, axes, 0, 0, axis_index_groups=groups, tiled=True)
+def exchanged(x, axis, first=0):
+    size = lax.axis_size(axis)
+    order = [(i + first) % size for i in range(size)]
+    return lax.all_to_all(x, axis, 0, 0, axis_index_groups=[order], tiled=True)
 
 
 def call(kernel, outs, *args, flops=0, scratch=(), outside=()):
@@ -232,7 +232,7 @@
     gain = norm_gain.reshape(1, width)
     block = shaped((taps, width), BF16)
     peers = lax.axis_size("chan")
-    near, far = lax.axis_size(NEAR), lax.axis_size(FAR)
+    near, far = lax.axis_size("near"), lax.axis_size("far")
     conv_flops = 4 * groups * taps * taps * LANES
 
     signal = (key_in.astype(F32) * value_in.astype(F32)).astype(BF16)
@@ -264,13 +264,12 @@
         sums, mixed, held, scaled, before, mirror,
         flops=conv_flops,
     )
-    totals = exchanged(totals, NEAR)
+    totals = exchanged(totals, "near", near // 4)
     (totals,) = call(gather_sum_kernel, [shaped((far, groups // near, taps), F32)], totals)
-    order = [(i + far // 2) % far for i in range(far)]
-    totals = exchanged(totals, FAR, [order])
+    totals = exchanged(totals, "far", far // 2)
     after = shifted(conv, CTX, -1)
     (totals,) = call(gather_sum_kernel, [shaped((near, groups // near, taps), F32)], totals)
-    grad_filters = exchanged(totals, NEAR).reshape(groups, taps)
+    grad_filters = exchanged(totals, "near", near // 4).reshape(groups, taps)
     normed, grad_query = call(
         output_kernel, [block, block], sums, mixed, held, scaled, gain
     )
@@ -284,7 +283,7 @@
 
 def solution(mesh):
     torus = Mesh(
-        mesh.devices.reshape(8, 4, 4, mesh.shape["chan"]), ("zh", "zl", "y", "chan")
+        mesh.devices.reshape(8, 16, mesh.shape["chan"]), ("far", "near", "chan")
     )
     rows = P(None, CTX, "chan")
     in_specs = (rows, rows, rows, rows, P("chan", None), P("chan"))

time: 91.9 us -> 91.2 us (level)
  waiting for transfers between devices: 7.55 us -> 5.99 us
    all_to_all x2, waiting for transfers between devices: 4.37 us -> 3.31 us  [exchanged(): return lax.all_to_all(x, axis, 0, 0, axis_index_groups=[order], tiled=True)]
  transfers between devices with their start and end apart: 4 -> 4, of which waited for: 4 -> 3; matrix products, arithmetic and copies ran while one was open for 0% -> 0% of each run, Pallas kernels for 9% -> 9%
where the time goes in v5:
time: 91.2 us; the launch traced here: 90.8 us
  starting transfers between devices  39.6 us (43%)
  blocking collectives  27.3 us (30%)
  Pallas kernels  15.5 us (17%)
  waiting for transfers between devices  5.99 us (7%)
  other arithmetic  1.1 us (1%)
    all_to_all x2, starting transfers between devices, exchanged(): return lax.all_to_all(x, axis, 0, 0, axis_index_groups=[order], tiled=True)  34.8 us
    all_to_all x2, blocking collectives, exchanged(): return lax.all_to_all(x, axis, 0, 0, axis_index_groups=[order], tiled=True)  27.3 us
    pallas_call x7, Pallas kernels, call(): pl.pallas_call(kernel, out_shape=outs, in_specs=[hbm if i in outside else...  15.5 us
    ppermute x2, starting transfers between devices, shifted(): return lax.ppermute(block, axes, route)  4.78 us
    all_to_all x2, waiting for transfers between devices, exchanged(): return lax.all_to_all(x, axis, 0, 0, axis_index_groups=[order], tiled=True)  3.31 us
    ppermute x2, waiting for transfers between devices, shifted(): return lax.ppermute(block, axes, route)  2.68 us
  transfers between devices with their start and end apart: 4, of which 3 were waited for; matrix products, arithmetic and copies ran while one was open for 0% of the time, Pallas kernels for 9%

profile of v5, /device:TPU:2, one launch (start us, length us, event | category | flops | bytes accessed | tf_op | source)
XLA Modules:
  0.0 90.8 jit_solution(391702514474204729)
XLA Ops:
  0.6 1.1 %multiply_convert_fusion.signal_ref = bf16[128,1024]{1,0:T(8,128)(2,1)S(1)} fusion(bf16[1,128,1024]{2,1,0:T(8,128)(2,1)} %param.8, bf16[1,128,1024]{2,1,0:T(8,128)(2,1)} %param.7), kind=kLoop, calls=%fused_computation | loop fusion | flops 524288 | bytes 786432 | tf_op jit(solution)/shard_map/convert_element_type | solution.py:238
  1.7 3.5 %collective-permute-start = (bf16[128,1024]{1,0:T(8,128)(2,1)S(1)}, bf16[128,1024]{1,0:T(8,128)(2,1)S(1)}, u32[]{:S(2)}, u32[]{:S(2)}) collective-permute-start(bf16[128,1024]{1,0:T(8,128)(2,1)S(1)} %multiply_convert_fusion.signal_ref), channel_id=1, source_target_pairs={{0,8},{8,16},{16,24},{24,32},{32,40},{40,48},{48,56},{56,64},{64,7... | collective-permute-start | bytes 786440 | tf_op jit(solution)/shard_map/ppermute | solution.py:23
  5.2 0.0 copy-start.3
  5.2 2.8 %shard_map.101 = (bf16[64,128,256]{2,1,0:T(8,128)(2,1)S(1)}, bf16[128,1024]{1,0:T(8,128)(2,1)S(1)}, bf16[128,1024]{1,0:T(8,128)(2,1)S(1)}, f32[128,1024]{1,0:T(8,128)S(1)}) custom-call(f32[64,128]{1,0:T(8,128)} %filters_ref.3, bf16[128,1024]{1,0:T(8,128)(2,1)S(1)} %multiply_convert_fusion.signal_ref, bf16[128,1024]{1,0:T(8,128)(2,1)} %bitcast.16, ...), custom_call_target="tpu_custom_call" | custom-call | bytes 6066176 | tf_op jit(solution)/shard_map/pallas_call | solution.py:41
  8.1 2.7 %collective-permute-done.before_ref = bf16[128,1024]{1,0:T(8,128)(2,1)S(1)} collective-permute-done((bf16[128,1024]{1,0:T(8,128)(2,1)S(1)}, bf16[128,1024]{1,0:T(8,128)(2,1)S(1)}, u32[]{:S(2)}, u32[]{:S(2)}) %collective-permute-start) | collective-permute-done | bytes 262176 | tf_op jit(solution)/shard_map/ppermute | solution.py:23
  10.8 0.0 copy-start
  10.8 0.0 copy-start.1
  10.8 0.0 copy-start.2
  10.8 2.5 %shard_map.102 = (f32[128,1024]{1,0:T(8,128)S(1)}, f32[8,2,128]{2,1,0:T(2,128)S(1)}) custom-call(bf16[64,128,256]{2,1,0:T(8,128)(2,1)S(1)} %get-tuple-element.20.weights_ref, bf16[128,1024]{1,0:T(8,128)(2,1)S(1)} %collective-permute-done.before_ref, bf16[128,1024]{1,0:T(8,128)(2,1)S(1)} %multiply_convert_fusion.signal_ref, ...), custom_call_target="tpu_custom_call" | custom-call | flops 536870912 | bytes 6037504 | tf_op jit(solution)/shard_map/pallas_call | solution.py:41
  13.2 15.5 %all_to_all.20.sums_ref = f32[8,2,128]{2,1,0:T(2,128)S(1)} all-to-all(f32[8,2,128]{2,1,0:T(2,128)S(1)} %get-tuple-element.23), channel_id=1, replica_groups={{0,1,2,3,4,5,6,7},{8,9,10,11,12,13,14,15},{16,17,18,19,20,21,22,23},{24..., dimensions={0} | all-to-all | bytes 16384 | tf_op jit(solution)/shard_map/all_to_all | solution.py:29
  28.8 4.3 %shard_map.103 = (bf16[128,1024]{1,0:T(8,128)(2,1)S(1)}, f32[16,4,128]{2,1,0:T(4,128)S(1)}) custom-call(f32[8,2,128]{2,1,0:T(2,128)S(1)} %all_to_all.20.sums_ref, f32[128,1024]{1,0:T(8,128)S(1)} %get-tuple-element.24.mixed_ref, bf16[128,1024]{1,0:T(8,128)(2,1)S(1)} %get-tuple-element.21.query_ref, f32[128,1024]{1,0:T(8,128)S(1)} %get-tuple-element.22.scaled_ref, ...), custom_call_target="tpu_custom_call" | custom-call | flops 536870912 | bytes 2138112 | tf_op jit(solution)/shard_map/pallas_call | solution.py:41
  33.1 11.8 %all_to_all.21.parts_ref = f32[16,4,128]{2,1,0:T(4,128)S(1)} all-to-all(f32[16,4,128]{2,1,0:T(4,128)S(1)} %get-tuple-element.34), channel_id=1, replica_groups={{32,40,48,56,64,72,80,88,96,104,112,120,0,8,16,24},{33,41,49,57,65,73,8..., dimensions={0} | all-to-all | bytes 65536 | tf_op jit(solution)/shard_map/all_to_all | solution.py:29
  44.9 0.6 shard_map.106
  45.5 29.6 %all-to-all-start.2 = ((f32[8,4,128]{2,1,0:T(4,128)}), f32[8,4,128]{2,1,0:T(4,128)S(1)}, u32[]{:S(2)}, u32[]{:S(2)}) async-start(f32[8,4,128]{2,1,0:T(4,128)} %shard_map.106), calls=%async_computation.2 | async-start | bytes 32768 | tf_op jit(solution)/shard_map/all_to_all | solution.py:29
  75.1 1.3 %collective-permute-start.1 = (bf16[128,1024]{1,0:T(8,128)(2,1)S(1)}, bf16[128,1024]{1,0:T(8,128)(2,1)S(1)}, u32[]{:S(2)}, u32[]{:S(2)}) collective-permute-start(bf16[128,1024]{1,0:T(8,128)(2,1)S(1)} %get-tuple-element.26.conv_ref), channel_id=1, source_target_pairs={{8,0},{16,8},{24,16},{32,24},{40,32},{48,40},{56,48},{64,56},{72,6... | collective-permute-start | bytes 786440 | tf_op jit(solution)/shard_map/ppermute | solution.py:23
  76.4 1.2 %all-to-all-done.2.parts_ref = f32[8,4,128]{2,1,0:T(4,128)S(1)} async-done(((f32[8,4,128]{2,1,0:T(4,128)}), f32[8,4,128]{2,1,0:T(4,128)S(1)}, u32[]{:S(2)}, u32[]{:S(2)}) %all-to-all-start.2) | async-done | bytes 16416 | tf_op jit(solution)/shard_map/all_to_all | solution.py:29
  77.6 0.6 shard_map.107
  78.3 5.2 %all-to-all-start.3 = ((f32[16,4,128]{2,1,0:T(4,128)}), f32[16,4,128]{2,1,0:T(4,128)S(1)}, u32[]{:S(2)}, u32[]{:S(2)}) async-start(f32[16,4,128]{2,1,0:T(4,128)} %shard_map.107), calls=%async_computation.3 | async-start | bytes 65536 | tf_op jit(solution)/shard_map/all_to_all | solution.py:29
  83.4 0.0 copy-done.3
  83.4 1.0 %shard_map.104 = (bf16[128,1024]{1,0:T(8,128)(2,1)}, bf16[128,1024]{1,0:T(8,128)(2,1)}) custom-call(f32[8,2,128]{2,1,0:T(2,128)S(1)} %all_to_all.20.sums_ref, f32[128,1024]{1,0:T(8,128)S(1)} %get-tuple-element.24.mixed_ref, bf16[128,1024]{1,0:T(8,128)(2,1)S(1)} %get-tuple-element.21.query_ref, f32[128,1024]{1,0:T(8,128)S(1)} %get-tuple-element.22.scaled_ref, ...), custom_call_target="tpu_custom_call" | custom-call | bytes 1847296 | tf_op jit(solution)/shard_map/pallas_call | solution.py:41
  84.5 0.0 collective-permute-done.1.after_ref
  84.5 0.0 copy-done
  84.5 0.0 copy-done.1
  84.5 0.0 copy-done.2
  84.5 3.6 %shard_map.105 = (bf16[128,1024]{1,0:T(8,128)(2,1)}, bf16[128,1024]{1,0:T(8,128)(2,1)}) custom-call(f32[64,128]{1,0:T(8,128)S(1)} %copy-done.2, bf16[128,1024]{1,0:T(8,128)(2,1)S(1)} %get-tuple-element.26.conv_ref, bf16[128,1024]{1,0:T(8,128)(2,1)S(1)} %collective-permute-done.1.after_ref, bf16[128,1024]{1,0:T(8,128)(2,1)S(1)} %bitcast.13, ...), custom_call_target="tpu_custom_call" | custom-call | flops 536870912 | bytes 1605632 | tf_op jit(solution)/shard_map/pallas_call | solution.py:41
  88.1 2.1 %all-to-all-done.3 = f32[16,4,128]{2,1,0:T(4,128)S(1)} async-done(((f32[16,4,128]{2,1,0:T(4,128)}), f32[16,4,128]{2,1,0:T(4,128)S(1)}, u32[]{:S(2)}, u32[]{:S(2)}) %all-to-all-start.3) | async-done | bytes 32800 | tf_op jit(solution)/shard_map/all_to_all | solution.py:29
  90.2 0.6 copy.12
Async XLA Ops:
  1.7 9.0 %collective-permute-start = (bf16[128,1024]{1,0:T(8,128)(2,1)S(1)}, bf16[128,1024]{1,0:T(8,128)(2,1)S(1)}, u32[]{:S(2)}, u32[]{:S(2)}) collective-permute-start(bf16[128,1024]{1,0:T(8,128)(2,1)S(1)} %multiply_convert_fusion.signal_ref), channel_id=1, source_target_pairs={{0,8},{8,16},{16,24},{24,32},{32,40},{40,48},{48,56},{56,64},{64,7... | collective-permute-start | bytes 786440 | tf_op jit(solution)/shard_map/ppermute | solution.py:23
  5.2 78.2 %copy-start.3 = (f32[1024]{0:T(1024)S(1)}, f32[1024]{0:T(1024)}, u32[]{:S(2)}) copy-start(f32[1024]{0:T(1024)} %param.11) | copy-start | bytes 12292
  10.8 73.7 %copy-start = (bf16[1,128,1024]{2,1,0:T(8,128)(2,1)S(1)}, bf16[1,128,1024]{2,1,0:T(8,128)(2,1)}, u32[]{:S(2)}) copy-start(bf16[1,128,1024]{2,1,0:T(8,128)(2,1)} %param.8) | copy-start | bytes 786436
  10.8 73.7 %copy-start.1 = (bf16[1,128,1024]{2,1,0:T(8,128)(2,1)S(1)}, bf16[1,128,1024]{2,1,0:T(8,128)(2,1)}, u32[]{:S(2)}) copy-start(bf16[1,128,1024]{2,1,0:T(8,128)(2,1)} %param.7) | copy-start | bytes 786436
  10.8 73.7 %copy-start.2 = (f32[64,128]{1,0:T(8,128)S(1)}, f32[64,128]{1,0:T(8,128)}, u32[]{:S(2)}) copy-start(f32[64,128]{1,0:T(8,128)} %filters_ref.3) | copy-start | bytes 98308
  45.5 32.1 %all-to-all-start.2 = ((f32[8,4,128]{2,1,0:T(4,128)}), f32[8,4,128]{2,1,0:T(4,128)S(1)}, u32[]{:S(2)}, u32[]{:S(2)}) async-start(f32[8,4,128]{2,1,0:T(4,128)} %shard_map.106), calls=%async_computation.2 | async-start | bytes 32768 | tf_op jit(solution)/shard_map/all_to_all | solution.py:29
  75.1 9.4 %collective-permute-start.1 = (bf16[128,1024]{1,0:T(8,128)(2,1)S(1)}, bf16[128,1024]{1,0:T(8,128)(2,1)S(1)}, u32[]{:S(2)}, u32[]{:S(2)}) collective-permute-start(bf16[128,1024]{1,0:T(8,128)(2,1)S(1)} %get-tuple-element.26.conv_ref), channel_id=1, source_target_pairs={{8,0},{16,8},{24,16},{32,24},{40,32},{48,40},{56,48},{64,56},{72,6... | collective-permute-start | bytes 786440 | tf_op jit(solution)/shard_map/ppermute | solution.py:23
  78.3 11.9 %all-to-all-start.3 = ((f32[16,4,128]{2,1,0:T(4,128)}), f32[16,4,128]{2,1,0:T(4,128)S(1)}, u32[]{:S(2)}, u32[]{:S(2)}) async-start(f32[16,4,128]{2,1,0:T(4,128)} %shard_map.107), calls=%async_computation.3 | async-start | bytes 65536 | tf_op jit(solution)/shard_map/all_to_all | solution.py:29

commit v6 on v5

--- a/solution.py
+++ b/solution.py
@@ -25,8 +25,8 @@
 
 def exchanged(x, axis, first=0):
     size = lax.axis_size(axis)
-    order = [(i + first) % size for i in range(size)]
-    return lax.all_to_all(x, axis, 0, 0, axis_index_groups=[order], tiled=True)
+    order = [[(i + first) % size for i in range(size)]] if first else None
+    return lax.all_to_all(x, axis, 0, 0, axis_index_groups=order, tiled=True)
 
 
 def call(kernel, outs, *args, flops=0, scratch=(), outside=()):
@@ -95,7 +95,7 @@
         weights_ref[g, :, taps:] = jnp.where(own, c, 0.0).astype(BF16)
         return 0
 
-    lax.fori_loop(0, groups, step, 0, unroll=4)
+    lax.fori_loop(0, groups, step, 0, unroll=8)
     for copy in copies[1:]:
         copy.wait()
     scaled_ref[...] = gain_copy[...] * cot_copy[...].astype(F32)
@@ -120,7 +120,7 @@
         return totals[0] + lifted * lifted, totals[1] + scaled_ref[:, lanes] * lifted
 
     zero = jnp.zeros((taps, LANES), F32)
-    power, inner = lax.fori_loop(0, width // LANES, step, (zero, zero))
+    power, inner = lax.fori_loop(0, width // LANES, step, (zero, zero), unroll=8)
     sums = jnp.concatenate(
         [jnp.sum(power.T, axis=0, keepdims=True), jnp.sum(inner.T, axis=0, keepdims=True)], axis=0
     )
@@ -171,7 +171,7 @@
             )
         return 0
 
-    lax.fori_loop(0, width // LANES, step, 0)
+    lax.fori_loop(0, width // LANES, step, 0, unroll=8)
 
 
 def output_kernel(
@@ -216,7 +216,7 @@
         value_grad_ref[:, lanes] = (acc * key_ref[:, lanes].astype(F32)).astype(BF16)
         return 0
 
-    lax.fori_loop(0, width // LANES, step, 0)
+    lax.fori_loop(0, width // LANES, step, 0, unroll=8)
 
 
 def gather_sum_kernel(parts_ref, out_ref):
@@ -264,12 +264,12 @@
         sums, mixed, held, scaled, before, mirror,
         flops=conv_flops,
     )
-    totals = exchanged(totals, "near", near // 4)
+    totals = exchanged(totals, "near")
     (totals,) = call(gather_sum_kernel, [shaped((far, groups // near, taps), F32)], totals)
     totals = exchanged(totals, "far", far // 2)
     after = shifted(conv, CTX, -1)
     (totals,) = call(gather_sum_kernel, [shaped((near, groups // near, taps), F32)], totals)
-    grad_filters = exchanged(totals, "near", near // 4).reshape(groups, taps)
+    grad_filters = exchanged(totals, "near").reshape(groups, taps)
     normed, grad_query = call(
         output_kernel, [block, block], sums, mixed, held, scaled, gain
     )
@@ -283,7 +283,7 @@
 
 def solution(mesh):
     torus = Mesh(
-        mesh.devices.reshape(8, 16, mesh.shape["chan"]), ("far", "near", "chan")
+        mesh.devices.reshape(16, 8, mesh.shape["chan"]), ("far", "near", "chan")
     )
     rows = P(None, CTX, "chan")
     in_specs = (rows, rows, rows, rows, P("chan", None), P("chan"))

time: 91.2 us -> 87.8 us (0.963)
  Pallas kernels: 15.5 us -> 10.8 us
  waiting for transfers between devices: 5.99 us -> 10.3 us
  blocking collectives: 27.3 us -> 25.3 us
  starting transfers between devices: 39.6 us -> 38.5 us
    pallas_call x7, Pallas kernels: 15.5 us -> 10.8 us  [call(): pl.pallas_call(kernel, out_shape=outs, in_specs=[hbm if i in outside else...]
    all_to_all x2, waiting for transfers between devices: 3.31 us -> 7.06 us  [exchanged(): return lax.all_to_all(x, axis, 0, 0, axis_index_groups=order, tiled=True)]
    all_to_all x2, blocking collectives: 27.3 us -> 25.3 us  [exchanged(): return lax.all_to_all(x, axis, 0, 0, axis_index_groups=order, tiled=True)]
    all_to_all x2, starting transfers between devices: 34.8 us -> 33.7 us  [exchanged(): return lax.all_to_all(x, axis, 0, 0, axis_index_groups=order, tiled=True)]
  transfers between devices with their start and end apart: 4 -> 4, of which waited for: 3 -> 3; matrix products, arithmetic and copies ran while one was open for 0% -> 0% of each run, Pallas kernels for 9% -> 7%
where the time goes in v6:
time: 87.8 us; the launch traced here: 87.4 us
  starting transfers between devices  38.5 us (44%)
  blocking collectives  25.3 us (29%)
  Pallas kernels  10.8 us (12%)
  waiting for transfers between devices  10.3 us (12%)
  other arithmetic  1.1 us (1%)
    all_to_all x2, starting transfers between devices, exchanged(): return lax.all_to_all(x, axis, 0, 0, axis_index_groups=order, tiled=True)  33.7 us
    all_to_all x2, blocking collectives, exchanged(): return lax.all_to_all(x, axis, 0, 0, axis_index_groups=order, tiled=True)  25.3 us
    pallas_call x7, Pallas kernels, call(): pl.pallas_call(kernel, out_shape=outs, in_specs=[hbm if i in outside else...  10.8 us
    all_to_all x2, waiting for transfers between devices, exchanged(): return lax.all_to_all(x, axis, 0, 0, axis_index_groups=order, tiled=True)  7.06 us
    ppermute x2, starting transfers between devices, shifted(): return lax.ppermute(block, axes, route)  4.78 us
    ppermute x2, waiting for transfers between devices, shifted(): return lax.ppermute(block, axes, route)  3.26 us
  transfers between devices with their start and end apart: 4, of which 3 were waited for; matrix products, arithmetic and copies ran while one was open for 0% of the time, Pallas kernels for 7%

profile of v6, /device:TPU:2, one launch (start us, length us, event | category | flops | bytes accessed | tf_op | source)
XLA Modules:
  0.0 87.4 jit_solution(14604999782241136728)
XLA Ops:
  0.6 1.1 %multiply_convert_fusion.signal_ref = bf16[128,1024]{1,0:T(8,128)(2,1)S(1)} fusion(bf16[1,128,1024]{2,1,0:T(8,128)(2,1)} %param.8, bf16[1,128,1024]{2,1,0:T(8,128)(2,1)} %param.7), kind=kLoop, calls=%fused_computation | loop fusion | flops 524288 | bytes 786432 | tf_op jit(solution)/shard_map/convert_element_type | solution.py:238
  1.7 3.5 %collective-permute-start = (bf16[128,1024]{1,0:T(8,128)(2,1)S(1)}, bf16[128,1024]{1,0:T(8,128)(2,1)S(1)}, u32[]{:S(2)}, u32[]{:S(2)}) collective-permute-start(bf16[128,1024]{1,0:T(8,128)(2,1)S(1)} %multiply_convert_fusion.signal_ref), channel_id=1, source_target_pairs={{0,8},{8,16},{16,24},{24,32},{32,40},{40,48},{48,56},{56,64},{64,7... | collective-permute-start | bytes 786440 | tf_op jit(solution)/shard_map/ppermute | solution.py:23
  5.2 2.3 %shard_map.101 = (bf16[64,128,256]{2,1,0:T(8,128)(2,1)S(1)}, bf16[128,1024]{1,0:T(8,128)(2,1)S(1)}, bf16[128,1024]{1,0:T(8,128)(2,1)S(1)}, f32[128,1024]{1,0:T(8,128)S(1)}) custom-call(f32[64,128]{1,0:T(8,128)} %filters_ref.3, bf16[128,1024]{1,0:T(8,128)(2,1)S(1)} %multiply_convert_fusion.signal_ref, bf16[128,1024]{1,0:T(8,128)(2,1)} %bitcast.16, ...), custom_call_target="tpu_custom_call" | custom-call | bytes 6066176 | tf_op jit(solution)/shard_map/pallas_call | solution.py:41
  7.5 0.0 copy-start.3
  7.5 3.3 %collective-permute-done.before_ref = bf16[128,1024]{1,0:T(8,128)(2,1)S(1)} collective-permute-done((bf16[128,1024]{1,0:T(8,128)(2,1)S(1)}, bf16[128,1024]{1,0:T(8,128)(2,1)S(1)}, u32[]{:S(2)}, u32[]{:S(2)}) %collective-permute-start) | collective-permute-done | bytes 262176 | tf_op jit(solution)/shard_map/ppermute | solution.py:23
  10.8 0.0 copy-start
  10.8 0.0 copy-start.1
  10.8 0.0 copy-start.2
  10.8 1.3 %shard_map.102 = (f32[128,1024]{1,0:T(8,128)S(1)}, f32[8,2,128]{2,1,0:T(2,128)S(1)}) custom-call(bf16[64,128,256]{2,1,0:T(8,128)(2,1)S(1)} %get-tuple-element.20.weights_ref, bf16[128,1024]{1,0:T(8,128)(2,1)S(1)} %collective-permute-done.before_ref, bf16[128,1024]{1,0:T(8,128)(2,1)S(1)} %multiply_convert_fusion.signal_ref, ...), custom_call_target="tpu_custom_call" | custom-call | flops 536870912 | bytes 6037504 | tf_op jit(solution)/shard_map/pallas_call | solution.py:41
  12.1 15.5 %all_to_all.20.sums_ref = f32[8,2,128]{2,1,0:T(2,128)S(1)} all-to-all(f32[8,2,128]{2,1,0:T(2,128)S(1)} %get-tuple-element.23), channel_id=1, replica_groups=mesh['far'=16,'near'=8,'chan'=8] {'chan'}, dimensions={0} | all-to-all | bytes 16384 | tf_op jit(solution)/shard_map/all_to_all | solution.py:29
  27.6 2.8 %shard_map.103 = (bf16[128,1024]{1,0:T(8,128)(2,1)S(1)}, f32[8,8,128]{2,1,0:T(8,128)S(1)}) custom-call(f32[8,2,128]{2,1,0:T(2,128)S(1)} %all_to_all.20.sums_ref, f32[128,1024]{1,0:T(8,128)S(1)} %get-tuple-element.24.mixed_ref, bf16[128,1024]{1,0:T(8,128)(2,1)S(1)} %get-tuple-element.21.query_ref, f32[128,1024]{1,0:T(8,128)S(1)} %get-tuple-element.22.scaled_ref, ...), custom_call_target="tpu_custom_call" | custom-call | flops 536870912 | bytes 2138112 | tf_op jit(solution)/shard_map/pallas_call | solution.py:41
  30.4 9.8 %all_to_all.21.parts_ref = f32[8,8,128]{2,1,0:T(8,128)S(1)} all-to-all(f32[8,8,128]{2,1,0:T(8,128)S(1)} %get-tuple-element.34), channel_id=1, replica_groups=mesh['far'=16,'near'=8,'chan'=8] {'near'}, dimensions={0} | all-to-all | bytes 65536 | tf_op jit(solution)/shard_map/all_to_all | solution.py:29
  40.2 0.6 shard_map.106
  40.8 30.4 %all-to-all-start.2 = ((f32[16,8,128]{2,1,0:T(8,128)}), f32[16,8,128]{2,1,0:T(8,128)S(1)}, u32[]{:S(2)}, u32[]{:S(2)}) async-start(f32[16,8,128]{2,1,0:T(8,128)} %shard_map.106), calls=%async_computation.2 | async-start | bytes 131072 | tf_op jit(solution)/shard_map/all_to_all | solution.py:29
  71.2 1.3 %collective-permute-start.1 = (bf16[128,1024]{1,0:T(8,128)(2,1)S(1)}, bf16[128,1024]{1,0:T(8,128)(2,1)S(1)}, u32[]{:S(2)}, u32[]{:S(2)}) collective-permute-start(bf16[128,1024]{1,0:T(8,128)(2,1)S(1)} %get-tuple-element.26.conv_ref), channel_id=1, source_target_pairs={{8,0},{16,8},{24,16},{32,24},{40,32},{48,40},{56,48},{64,56},{72,6... | collective-permute-start | bytes 786440 | tf_op jit(solution)/shard_map/ppermute | solution.py:23
  72.5 4.1 %all-to-all-done.2.parts_ref = f32[16,8,128]{2,1,0:T(8,128)S(1)} async-done(((f32[16,8,128]{2,1,0:T(8,128)}), f32[16,8,128]{2,1,0:T(8,128)S(1)}, u32[]{:S(2)}, u32[]{:S(2)}) %all-to-all-start.2) | async-done | bytes 65568 | tf_op jit(solution)/shard_map/all_to_all | solution.py:29
  76.6 0.6 shard_map.107
  77.2 3.3 %all-to-all-start.3 = ((f32[8,8,128]{2,1,0:T(8,128)}), f32[8,8,128]{2,1,0:T(8,128)S(1)}, u32[]{:S(2)}, u32[]{:S(2)}) async-start(f32[8,8,128]{2,1,0:T(8,128)} %shard_map.107), calls=%async_computation.3 | async-start | bytes 65536 | tf_op jit(solution)/shard_map/all_to_all | solution.py:29
  80.6 0.0 copy-done.3
  80.6 1.0 %shard_map.104 = (bf16[128,1024]{1,0:T(8,128)(2,1)}, bf16[128,1024]{1,0:T(8,128)(2,1)}) custom-call(f32[8,2,128]{2,1,0:T(2,128)S(1)} %all_to_all.20.sums_ref, f32[128,1024]{1,0:T(8,128)S(1)} %get-tuple-element.24.mixed_ref, bf16[128,1024]{1,0:T(8,128)(2,1)S(1)} %get-tuple-element.21.query_ref, f32[128,1024]{1,0:T(8,128)S(1)} %get-tuple-element.22.scaled_ref, ...), custom_call_target="tpu_custom_call" | custom-call | bytes 1847296 | tf_op jit(solution)/shard_map/pallas_call | solution.py:41
  81.6 0.0 collective-permute-done.1.after_ref
  81.6 0.0 copy-done
  81.6 0.0 copy-done.1
  81.6 0.0 copy-done.2
  81.6 2.1 %shard_map.105 = (bf16[128,1024]{1,0:T(8,128)(2,1)}, bf16[128,1024]{1,0:T(8,128)(2,1)}) custom-call(f32[64,128]{1,0:T(8,128)S(1)} %copy-done.2, bf16[128,1024]{1,0:T(8,128)(2,1)S(1)} %get-tuple-element.26.conv_ref, bf16[128,1024]{1,0:T(8,128)(2,1)S(1)} %collective-permute-done.1.after_ref, bf16[128,1024]{1,0:T(8,128)(2,1)S(1)} %bitcast.13, ...), custom_call_target="tpu_custom_call" | custom-call | flops 536870912 | bytes 1605632 | tf_op jit(solution)/shard_map/pallas_call | solution.py:41
  83.8 3.0 %all-to-all-done.3 = f32[8,8,128]{2,1,0:T(8,128)S(1)} async-done(((f32[8,8,128]{2,1,0:T(8,128)}), f32[8,8,128]{2,1,0:T(8,128)S(1)}, u32[]{:S(2)}, u32[]{:S(2)}) %all-to-all-start.3) | async-done | bytes 32800 | tf_op jit(solution)/shard_map/all_to_all | solution.py:29
  86.8 0.6 copy.12
Async XLA Ops:
  1.7 9.0 %collective-permute-start = (bf16[128,1024]{1,0:T(8,128)(2,1)S(1)}, bf16[128,1024]{1,0:T(8,128)(2,1)S(1)}, u32[]{:S(2)}, u32[]{:S(2)}) collective-permute-start(bf16[128,1024]{1,0:T(8,128)(2,1)S(1)} %multiply_convert_fusion.signal_ref), channel_id=1, source_target_pairs={{0,8},{8,16},{16,24},{24,32},{32,40},{40,48},{48,56},{56,64},{64,7... | collective-permute-start | bytes 786440 | tf_op jit(solution)/shard_map/ppermute | solution.py:23
  7.5 73.1 %copy-start.3 = (f32[1024]{0:T(1024)S(1)}, f32[1024]{0:T(1024)}, u32[]{:S(2)}) copy-start(f32[1024]{0:T(1024)} %param.11) | copy-start | bytes 12292
  10.8 70.9 %copy-start = (bf16[1,128,1024]{2,1,0:T(8,128)(2,1)S(1)}, bf16[1,128,1024]{2,1,0:T(8,128)(2,1)}, u32[]{:S(2)}) copy-start(bf16[1,128,1024]{2,1,0:T(8,128)(2,1)} %param.8) | copy-start | bytes 786436
  10.8 70.9 %copy-start.1 = (bf16[1,128,1024]{2,1,0:T(8,128)(2,1)S(1)}, bf16[1,128,1024]{2,1,0:T(8,128)(2,1)}, u32[]{:S(2)}) copy-start(bf16[1,128,1024]{2,1,0:T(8,128)(2,1)} %param.7) | copy-start | bytes 786436
  10.8 70.9 %copy-start.2 = (f32[64,128]{1,0:T(8,128)S(1)}, f32[64,128]{1,0:T(8,128)}, u32[]{:S(2)}) copy-start(f32[64,128]{1,0:T(8,128)} %filters_ref.3) | copy-start | bytes 98308
  40.8 35.7 %all-to-all-start.2 = ((f32[16,8,128]{2,1,0:T(8,128)}), f32[16,8,128]{2,1,0:T(8,128)S(1)}, u32[]{:S(2)}, u32[]{:S(2)}) async-start(f32[16,8,128]{2,1,0:T(8,128)} %shard_map.106), calls=%async_computation.2 | async-start | bytes 131072 | tf_op jit(solution)/shard_map/all_to_all | solution.py:29
  71.2 10.4 %collective-permute-start.1 = (bf16[128,1024]{1,0:T(8,128)(2,1)S(1)}, bf16[128,1024]{1,0:T(8,128)(2,1)S(1)}, u32[]{:S(2)}, u32[]{:S(2)}) collective-permute-start(bf16[128,1024]{1,0:T(8,128)(2,1)S(1)} %get-tuple-element.26.conv_ref), channel_id=1, source_target_pairs={{8,0},{16,8},{24,16},{32,24},{40,32},{48,40},{56,48},{64,56},{72,6... | collective-permute-start | bytes 786440 | tf_op jit(solution)/shard_map/ppermute | solution.py:23
  77.2 9.5 %all-to-all-start.3 = ((f32[8,8,128]{2,1,0:T(8,128)}), f32[8,8,128]{2,1,0:T(8,128)S(1)}, u32[]{:S(2)}, u32[]{:S(2)}) async-start(f32[8,8,128]{2,1,0:T(8,128)} %shard_map.107), calls=%async_computation.3 | async-start | bytes 65536 | tf_op jit(solution)/shard_map/all_to_all | solution.py:29

commit v7 on v6

--- a/solution.py
+++ b/solution.py
@@ -220,7 +220,8 @@
 
 
 def gather_sum_kernel(parts_ref, out_ref):
-    out_ref[...] = jnp.broadcast_to(jnp.sum(parts_ref[...], axis=0)[None], out_ref.shape)
+    total = jnp.sum(parts_ref[...].astype(F32), axis=0).astype(out_ref.dtype)
+    out_ref[...] = jnp.broadcast_to(total[None], out_ref.shape)
 
 
 def body(query, key_in, value_in, cotangent, filters, norm_gain):
@@ -265,7 +266,7 @@
         flops=conv_flops,
     )
     totals = exchanged(totals, "near")
-    (totals,) = call(gather_sum_kernel, [shaped((far, groups // near, taps), F32)], totals)
+    (totals,) = call(gather_sum_kernel, [shaped((far, groups // near, taps), BF16)], totals)
     totals = exchanged(totals, "far", far // 2)
     after = shifted(conv, CTX, -1)
     (totals,) = call(gather_sum_kernel, [shaped((near, groups // near, taps), F32)], totals)

time: 87.8 us -> 86.1 us (0.981)
  waiting for transfers between devices: 10.3 us -> 8.67 us
    all_to_all x2, waiting for transfers between devices: 7.06 us -> 5.41 us  [exchanged(): return lax.all_to_all(x, axis, 0, 0, axis_index_groups=order, tiled=True)]
where the time goes in v7:
time: 86.1 us; the launch traced here: 85.7 us
  starting transfers between devices  38.5 us (45%)
  blocking collectives  25.3 us (29%)
  Pallas kernels  10.8 us (13%)
  waiting for transfers between devices  8.67 us (10%)
  other arithmetic  1.1 us (1%)
    all_to_all x2, starting transfers between devices, exchanged(): return lax.all_to_all(x, axis, 0, 0, axis_index_groups=order, tiled=True)  33.7 us
    all_to_all x2, blocking collectives, exchanged(): return lax.all_to_all(x, axis, 0, 0, axis_index_groups=order, tiled=True)  25.3 us
    pallas_call x7, Pallas kernels, call(): pl.pallas_call(kernel, out_shape=outs, in_specs=[hbm if i in outside else...  10.8 us
    all_to_all x2, waiting for transfers between devices, exchanged(): return lax.all_to_all(x, axis, 0, 0, axis_index_groups=order, tiled=True)  5.41 us
    ppermute x2, starting transfers between devices, shifted(): return lax.ppermute(block, axes, route)  4.78 us
    ppermute x2, waiting for transfers between devices, shifted(): return lax.ppermute(block, axes, route)  3.26 us
  transfers between devices with their start and end apart: 4, of which 3 were waited for; matrix products, arithmetic and copies ran while one was open for 0% of the time, Pallas kernels for 7%

profile of v7, /device:TPU:2, one launch (start us, length us, event | category | flops | bytes accessed | tf_op | source)
XLA Modules:
  0.0 85.7 jit_solution(8922896217325286870)
XLA Ops:
  0.6 1.1 %multiply_convert_fusion.signal_ref = bf16[128,1024]{1,0:T(8,128)(2,1)S(1)} fusion(bf16[1,128,1024]{2,1,0:T(8,128)(2,1)} %param.8, bf16[1,128,1024]{2,1,0:T(8,128)(2,1)} %param.7), kind=kLoop, calls=%fused_computation | loop fusion | flops 524288 | bytes 786432 | tf_op jit(solution)/shard_map/convert_element_type | solution.py:239
  1.7 3.5 %collective-permute-start = (bf16[128,1024]{1,0:T(8,128)(2,1)S(1)}, bf16[128,1024]{1,0:T(8,128)(2,1)S(1)}, u32[]{:S(2)}, u32[]{:S(2)}) collective-permute-start(bf16[128,1024]{1,0:T(8,128)(2,1)S(1)} %multiply_convert_fusion.signal_ref), channel_id=1, source_target_pairs={{0,8},{8,16},{16,24},{24,32},{32,40},{40,48},{48,56},{56,64},{64,7... | collective-permute-start | bytes 786440 | tf_op jit(solution)/shard_map/ppermute | solution.py:23
  5.2 0.0 copy-start.3
  5.2 2.3 %shard_map.101 = (bf16[64,128,256]{2,1,0:T(8,128)(2,1)S(1)}, bf16[128,1024]{1,0:T(8,128)(2,1)S(1)}, bf16[128,1024]{1,0:T(8,128)(2,1)S(1)}, f32[128,1024]{1,0:T(8,128)S(1)}) custom-call(f32[64,128]{1,0:T(8,128)} %filters_ref.3, bf16[128,1024]{1,0:T(8,128)(2,1)S(1)} %multiply_convert_fusion.signal_ref, bf16[128,1024]{1,0:T(8,128)(2,1)} %bitcast.16, ...), custom_call_target="tpu_custom_call" | custom-call | bytes 6066176 | tf_op jit(solution)/shard_map/pallas_call | solution.py:41
  7.5 3.3 %collective-permute-done.before_ref = bf16[128,1024]{1,0:T(8,128)(2,1)S(1)} collective-permute-done((bf16[128,1024]{1,0:T(8,128)(2,1)S(1)}, bf16[128,1024]{1,0:T(8,128)(2,1)S(1)}, u32[]{:S(2)}, u32[]{:S(2)}) %collective-permute-start) | collective-permute-done | bytes 262176 | tf_op jit(solution)/shard_map/ppermute | solution.py:23
  10.8 0.0 copy-start
  10.8 0.0 copy-start.1
  10.8 0.0 copy-start.2
  10.8 1.3 %shard_map.102 = (f32[128,1024]{1,0:T(8,128)S(1)}, f32[8,2,128]{2,1,0:T(2,128)S(1)}) custom-call(bf16[64,128,256]{2,1,0:T(8,128)(2,1)S(1)} %get-tuple-element.20.weights_ref, bf16[128,1024]{1,0:T(8,128)(2,1)S(1)} %collective-permute-done.before_ref, bf16[128,1024]{1,0:T(8,128)(2,1)S(1)} %multiply_convert_fusion.signal_ref, ...), custom_call_target="tpu_custom_call" | custom-call | flops 536870912 | bytes 6037504 | tf_op jit(solution)/shard_map/pallas_call | solution.py:41
  12.1 15.5 %all_to_all.20.sums_ref = f32[8,2,128]{2,1,0:T(2,128)S(1)} all-to-all(f32[8,2,128]{2,1,0:T(2,128)S(1)} %get-tuple-element.23), channel_id=1, replica_groups=mesh['far'=16,'near'=8,'chan'=8] {'chan'}, dimensions={0} | all-to-all | bytes 16384 | tf_op jit(solution)/shard_map/all_to_all | solution.py:29
  27.6 2.8 %shard_map.103 = (bf16[128,1024]{1,0:T(8,128)(2,1)S(1)}, f32[8,8,128]{2,1,0:T(8,128)S(1)}) custom-call(f32[8,2,128]{2,1,0:T(2,128)S(1)} %all_to_all.20.sums_ref, f32[128,1024]{1,0:T(8,128)S(1)} %get-tuple-element.24.mixed_ref, bf16[128,1024]{1,0:T(8,128)(2,1)S(1)} %get-tuple-element.21.query_ref, f32[128,1024]{1,0:T(8,128)S(1)} %get-tuple-element.22.scaled_ref, ...), custom_call_target="tpu_custom_call" | custom-call | flops 536870912 | bytes 2138112 | tf_op jit(solution)/shard_map/pallas_call | solution.py:41
  30.4 9.8 %all_to_all.21.parts_ref = f32[8,8,128]{2,1,0:T(8,128)S(1)} all-to-all(f32[8,8,128]{2,1,0:T(8,128)S(1)} %get-tuple-element.34), channel_id=1, replica_groups=mesh['far'=16,'near'=8,'chan'=8] {'near'}, dimensions={0} | all-to-all | bytes 65536 | tf_op jit(solution)/shard_map/all_to_all | solution.py:29
  40.2 0.6 shard_map.106
  40.8 30.4 %all-to-all-start.2 = ((bf16[16,8,128]{2,1,0:T(8,128)(2,1)}), bf16[16,8,128]{2,1,0:T(8,128)(2,1)S(1)}, u32[]{:S(2)}, u32[]{:S(2)}) async-start(bf16[16,8,128]{2,1,0:T(8,128)(2,1)} %shard_map.106), calls=%async_computation.2 | async-start | bytes 65536 | tf_op jit(solution)/shard_map/all_to_all | solution.py:29
  71.2 1.3 %collective-permute-start.1 = (bf16[128,1024]{1,0:T(8,128)(2,1)S(1)}, bf16[128,1024]{1,0:T(8,128)(2,1)S(1)}, u32[]{:S(2)}, u32[]{:S(2)}) collective-permute-start(bf16[128,1024]{1,0:T(8,128)(2,1)S(1)} %get-tuple-element.26.conv_ref), channel_id=1, source_target_pairs={{8,0},{16,8},{24,16},{32,24},{40,32},{48,40},{56,48},{64,56},{72,6... | collective-permute-start | bytes 786440 | tf_op jit(solution)/shard_map/ppermute | solution.py:23
  72.5 2.4 %all-to-all-done.2.parts_ref = bf16[16,8,128]{2,1,0:T(8,128)(2,1)S(1)} async-done(((bf16[16,8,128]{2,1,0:T(8,128)(2,1)}), bf16[16,8,128]{2,1,0:T(8,128)(2,1)S(1)}, u32[]{:S(2)}, u32[]{:S(2)}) %all-to-all-start.2) | async-done | bytes 32800 | tf_op jit(solution)/shard_map/all_to_all | solution.py:29
  74.9 0.6 shard_map.107
  75.6 3.3 %all-to-all-start.3 = ((f32[8,8,128]{2,1,0:T(8,128)}), f32[8,8,128]{2,1,0:T(8,128)S(1)}, u32[]{:S(2)}, u32[]{:S(2)}) async-start(f32[8,8,128]{2,1,0:T(8,128)} %shard_map.107), calls=%async_computation.3 | async-start | bytes 65536 | tf_op jit(solution)/shard_map/all_to_all | solution.py:29
  78.9 0.0 copy-done.3
  78.9 1.0 %shard_map.104 = (bf16[128,1024]{1,0:T(8,128)(2,1)}, bf16[128,1024]{1,0:T(8,128)(2,1)}) custom-call(f32[8,2,128]{2,1,0:T(2,128)S(1)} %all_to_all.20.sums_ref, f32[128,1024]{1,0:T(8,128)S(1)} %get-tuple-element.24.mixed_ref, bf16[128,1024]{1,0:T(8,128)(2,1)S(1)} %get-tuple-element.21.query_ref, f32[128,1024]{1,0:T(8,128)S(1)} %get-tuple-element.22.scaled_ref, ...), custom_call_target="tpu_custom_call" | custom-call | bytes 1847296 | tf_op jit(solution)/shard_map/pallas_call | solution.py:41
  80.0 0.0 collective-permute-done.1.after_ref
  80.0 0.0 copy-done
  80.0 0.0 copy-done.1
  80.0 0.0 copy-done.2
  80.0 2.1 %shard_map.105 = (bf16[128,1024]{1,0:T(8,128)(2,1)}, bf16[128,1024]{1,0:T(8,128)(2,1)}) custom-call(f32[64,128]{1,0:T(8,128)S(1)} %copy-done.2, bf16[128,1024]{1,0:T(8,128)(2,1)S(1)} %get-tuple-element.26.conv_ref, bf16[128,1024]{1,0:T(8,128)(2,1)S(1)} %collective-permute-done.1.after_ref, bf16[128,1024]{1,0:T(8,128)(2,1)S(1)} %bitcast.13, ...), custom_call_target="tpu_custom_call" | custom-call | flops 536870912 | bytes 1605632 | tf_op jit(solution)/shard_map/pallas_call | solution.py:41
  82.1 3.0 %all-to-all-done.3 = f32[8,8,128]{2,1,0:T(8,128)S(1)} async-done(((f32[8,8,128]{2,1,0:T(8,128)}), f32[8,8,128]{2,1,0:T(8,128)S(1)}, u32[]{:S(2)}, u32[]{:S(2)}) %all-to-all-start.3) | async-done | bytes 32800 | tf_op jit(solution)/shard_map/all_to_all | solution.py:29
  85.1 0.6 copy.12
Async XLA Ops:
  1.7 9.0 %collective-permute-start = (bf16[128,1024]{1,0:T(8,128)(2,1)S(1)}, bf16[128,1024]{1,0:T(8,128)(2,1)S(1)}, u32[]{:S(2)}, u32[]{:S(2)}) collective-permute-start(bf16[128,1024]{1,0:T(8,128)(2,1)S(1)} %multiply_convert_fusion.signal_ref), channel_id=1, source_target_pairs={{0,8},{8,16},{16,24},{24,32},{32,40},{40,48},{48,56},{56,64},{64,7... | collective-permute-start | bytes 786440 | tf_op jit(solution)/shard_map/ppermute | solution.py:23
  5.2 73.7 %copy-start.3 = (f32[1024]{0:T(1024)S(1)}, f32[1024]{0:T(1024)}, u32[]{:S(2)}) copy-start(f32[1024]{0:T(1024)} %param.11) | copy-start | bytes 12292
  10.8 69.2 %copy-start = (bf16[1,128,1024]{2,1,0:T(8,128)(2,1)S(1)}, bf16[1,128,1024]{2,1,0:T(8,128)(2,1)}, u32[]{:S(2)}) copy-start(bf16[1,128,1024]{2,1,0:T(8,128)(2,1)} %param.8) | copy-start | bytes 786436
  10.8 69.2 %copy-start.1 = (bf16[1,128,1024]{2,1,0:T(8,128)(2,1)S(1)}, bf16[1,128,1024]{2,1,0:T(8,128)(2,1)}, u32[]{:S(2)}) copy-start(bf16[1,128,1024]{2,1,0:T(8,128)(2,1)} %param.7) | copy-start | bytes 786436
  10.8 69.2 %copy-start.2 = (f32[64,128]{1,0:T(8,128)S(1)}, f32[64,128]{1,0:T(8,128)}, u32[]{:S(2)}) copy-start(f32[64,128]{1,0:T(8,128)} %filters_ref.3) | copy-start | bytes 98308
  40.8 34.1 %all-to-all-start.2 = ((bf16[16,8,128]{2,1,0:T(8,128)(2,1)}), bf16[16,8,128]{2,1,0:T(8,128)(2,1)S(1)}, u32[]{:S(2)}, u32[]{:S(2)}) async-start(bf16[16,8,128]{2,1,0:T(8,128)(2,1)} %shard_map.106), calls=%async_computation.2 | async-start | bytes 65536 | tf_op jit(solution)/shard_map/all_to_all | solution.py:29
  71.2 8.7 %collective-permute-start.1 = (bf16[128,1024]{1,0:T(8,128)(2,1)S(1)}, bf16[128,1024]{1,0:T(8,128)(2,1)S(1)}, u32[]{:S(2)}, u32[]{:S(2)}) collective-permute-start(bf16[128,1024]{1,0:T(8,128)(2,1)S(1)} %get-tuple-element.26.conv_ref), channel_id=1, source_target_pairs={{8,0},{16,8},{24,16},{32,24},{40,32},{48,40},{56,48},{64,56},{72,6... | collective-permute-start | bytes 786440 | tf_op jit(solution)/shard_map/ppermute | solution.py:23
  75.6 9.5 %all-to-all-start.3 = ((f32[8,8,128]{2,1,0:T(8,128)}), f32[8,8,128]{2,1,0:T(8,128)S(1)}, u32[]{:S(2)}, u32[]{:S(2)}) async-start(f32[8,8,128]{2,1,0:T(8,128)} %shard_map.107), calls=%async_computation.3 | async-start | bytes 65536 | tf_op jit(solution)/shard_map/all_to_all | solution.py:29

commit v8 on v7

--- a/solution.py
+++ b/solution.py
@@ -68,7 +68,7 @@
 
 def prepare_kernel(
     filters_ref, signal_ref, query_ref, cot_ref, gain_ref,
-    weights_ref, mirror_ref, held_ref, scaled_ref, taps_ref, back_taps_ref, cot_copy, gain_copy, sems,
+    weights_ref, near_ref, mirror_ref, held_ref, scaled_ref, own_ref, taps_ref, back_taps_ref, cot_copy, gain_copy, sems,
 ):
     groups, taps = filters_ref.shape
     copies = [
@@ -91,30 +91,47 @@
 
     def step(g, _):
         c = rolled(back_taps_ref[pl.ds(g, 1), :], taps)
-        weights_ref[g, :, :taps] = jnp.where(own, 0.0, c).astype(BF16)
-        weights_ref[g, :, taps:] = jnp.where(own, c, 0.0).astype(BF16)
+        weights_ref[g] = jnp.where(own, 0.0, c).astype(BF16)
+        own_ref[g] = jnp.where(own, c, 0.0).astype(BF16)
         return 0
 
     lax.fori_loop(0, groups, step, 0, unroll=8)
+    width = signal_ref.shape[1]
+    per_tile = groups * LANES // width
+    owner = index((taps, LANES), 1) // (LANES // per_tile)
+
+    def tile(i, _):
+        lanes = pl.ds(pl.multiple_of(i * LANES, LANES), LANES)
+        acc = None
+        for k in range(per_tile):
+            out = jnp.dot(
+                own_ref[i * per_tile + k], signal_ref[:, lanes], preferred_element_type=F32
+            )
+            acc = out if acc is None else jnp.where(owner == k, out, acc)
+        near_ref[:, lanes] = acc
+        return 0
+
+    lax.fori_loop(0, width // LANES, tile, 0, unroll=2)
     for copy in copies[1:]:
         copy.wait()
     scaled_ref[...] = gain_copy[...] * cot_copy[...].astype(F32)
 
 
-def mix_kernel(weights_ref, before_ref, signal_ref, query_ref, scaled_ref, mixed_ref, sums_ref):
+def mix_kernel(weights_ref, before_ref, near_ref, query_ref, scaled_ref, mixed_ref, sums_ref):
     groups, taps, _ = weights_ref.shape
-    width = signal_ref.shape[1]
+    width = before_ref.shape[1]
     per_tile = groups * LANES // width
     members = LANES // per_tile
     owner = index((taps, LANES), 1) // members
 
     def step(i, totals):
         lanes = pl.ds(pl.multiple_of(i * LANES, LANES), LANES)
-        window = jnp.concatenate([before_ref[:, lanes], signal_ref[:, lanes]], axis=0)
+        window = before_ref[:, lanes]
         acc = None
         for k in range(per_tile):
             out = jnp.dot(weights_ref[i * per_tile + k], window, preferred_element_type=F32)
             acc = out if acc is None else jnp.where(owner == k, out, acc)
+        acc = acc + near_ref[:, lanes]
         mixed_ref[:, lanes] = acc
         lifted = query_ref[:, lanes].astype(F32) * acc
         return totals[0] + lifted * lifted, totals[1] + scaled_ref[:, lanes] * lifted
@@ -239,11 +256,12 @@
     signal = (key_in.astype(F32) * value_in.astype(F32)).astype(BF16)
     before = shifted(signal, CTX, 1)
     wide = shaped((taps, width), F32)
-    weights, mirror, held, scaled = call(
+    weights, near_mixed, mirror, held, scaled = call(
         prepare_kernel,
-        [shaped((groups, taps, 2 * taps), BF16), block, block, wide],
+        [shaped((groups, taps, taps), BF16), wide, block, block, wide],
         filters, signal, query, cotangent, gain,
         scratch=[
+            pltpu.VMEM((groups, taps, taps), BF16),
             pltpu.VMEM((groups, taps), F32),
             pltpu.VMEM((groups, taps), F32),
             pltpu.VMEM((taps, width), BF16),
@@ -255,7 +273,7 @@
     mixed, sums = call(
         mix_kernel,
         [wide, shaped((peers, 2, taps), F32)],
-        weights, before, signal, held, scaled,
+        weights, before, near_mixed, held, scaled,
         flops=conv_flops,
     )
     sums = exchanged(sums, "chan")

time: 86.1 us -> 85.8 us (level)
  waiting for transfers between devices: 8.67 us -> 7.63 us
    ppermute x2, waiting for transfers between devices: 3.26 us -> 2.21 us  [shifted(): return lax.ppermute(block, axes, route)]
  transfers between devices with their start and end apart: 4 -> 4, of which waited for: 3 -> 3; matrix products, arithmetic and copies ran while one was open for 0% -> 0% of each run, Pallas kernels for 7% -> 8%
where the time goes in v8:
time: 85.8 us; the launch traced here: 85.4 us
  starting transfers between devices  38.5 us (45%)
  blocking collectives  25.5 us (30%)
  Pallas kernels  11.3 us (13%)
  waiting for transfers between devices  7.63 us (9%)
  other arithmetic  1.1 us (1%)
    all_to_all x2, starting transfers between devices, exchanged(): return lax.all_to_all(x, axis, 0, 0, axis_index_groups=order, tiled=True)  33.7 us
    all_to_all x2, blocking collectives, exchanged(): return lax.all_to_all(x, axis, 0, 0, axis_index_groups=order, tiled=True)  25.5 us
    pallas_call x7, Pallas kernels, call(): pl.pallas_call(kernel, out_shape=outs, in_specs=[hbm if i in outside else...  11.3 us
    all_to_all x2, waiting for transfers between devices, exchanged(): return lax.all_to_all(x, axis, 0, 0, axis_index_groups=order, tiled=True)  5.42 us
    ppermute x2, starting transfers between devices, shifted(): return lax.ppermute(block, axes, route)  4.78 us
    ppermute x2, waiting for transfers between devices, shifted(): return lax.ppermute(block, axes, route)  2.21 us
  transfers between devices with their start and end apart: 4, of which 3 were waited for; matrix products, arithmetic and copies ran while one was open for 0% of the time, Pallas kernels for 8%

profile of v8, /device:TPU:2, one launch (start us, length us, event | category | flops | bytes accessed | tf_op | source)
XLA Modules:
  0.0 85.4 jit_solution(5332850583405849287)
XLA Ops:
  0.6 1.1 %multiply_convert_fusion.signal_ref = bf16[128,1024]{1,0:T(8,128)(2,1)S(1)} fusion(bf16[1,128,1024]{2,1,0:T(8,128)(2,1)} %param.8, bf16[1,128,1024]{2,1,0:T(8,128)(2,1)} %param.7), kind=kLoop, calls=%fused_computation | loop fusion | flops 524288 | bytes 786432 | tf_op jit(solution)/shard_map/convert_element_type | solution.py:256
  1.7 3.5 %collective-permute-start = (bf16[128,1024]{1,0:T(8,128)(2,1)S(1)}, bf16[128,1024]{1,0:T(8,128)(2,1)S(1)}, u32[]{:S(2)}, u32[]{:S(2)}) collective-permute-start(bf16[128,1024]{1,0:T(8,128)(2,1)S(1)} %multiply_convert_fusion.signal_ref), channel_id=1, source_target_pairs={{0,8},{8,16},{16,24},{24,32},{32,40},{40,48},{48,56},{56,64},{64,7... | collective-permute-start | bytes 786440 | tf_op jit(solution)/shard_map/ppermute | solution.py:23
  5.2 3.3 %shard_map.101 = (bf16[64,128,128]{2,1,0:T(8,128)(2,1)S(1)}, f32[128,1024]{1,0:T(8,128)S(1)}, bf16[128,1024]{1,0:T(8,128)(2,1)S(1)}, bf16[128,1024]{1,0:T(8,128)(2,1)S(1)}, f32[128,1024]{1,0:T(8,128)S(1)}) custom-call(f32[64,128]{1,0:T(8,128)} %filters_ref.3, bf16[128,1024]{1,0:T(8,128)(2,1)S(1)} %multiply_convert_fusion.signal_ref, ...), custom_call_target="tpu_custom_call" | custom-call | bytes 4493312 | tf_op jit(solution)/shard_map/pallas_call | solution.py:41
  8.6 2.2 %collective-permute-done.before_ref = bf16[128,1024]{1,0:T(8,128)(2,1)S(1)} collective-permute-done((bf16[128,1024]{1,0:T(8,128)(2,1)S(1)}, bf16[128,1024]{1,0:T(8,128)(2,1)S(1)}, u32[]{:S(2)}, u32[]{:S(2)}) %collective-permute-start) | collective-permute-done | bytes 262176 | tf_op jit(solution)/shard_map/ppermute | solution.py:23
  10.8 0.0 copy-start.3
  10.8 0.9 %shard_map.102 = (f32[128,1024]{1,0:T(8,128)S(1)}, f32[8,2,128]{2,1,0:T(2,128)S(1)}) custom-call(bf16[64,128,128]{2,1,0:T(8,128)(2,1)S(1)} %get-tuple-element.21.weights_ref, bf16[128,1024]{1,0:T(8,128)(2,1)S(1)} %collective-permute-done.before_ref, f32[128,1024]{1,0:T(8,128)S(1)} %get-tuple-element.22.near_ref, ...), custom_call_target="tpu_custom_call" | custom-call | flops 536870912 | bytes 4202496 | tf_op jit(solution)/shard_map/pallas_call | solution.py:41
  11.6 0.0 copy-start
  11.7 0.0 copy-start.1
  11.7 0.0 copy-start.2
  11.7 15.6 %all_to_all.20.sums_ref = f32[8,2,128]{2,1,0:T(2,128)S(1)} all-to-all(f32[8,2,128]{2,1,0:T(2,128)S(1)} %get-tuple-element.25), channel_id=1, replica_groups=mesh['far'=16,'near'=8,'chan'=8] {'chan'}, dimensions={0} | all-to-all | bytes 16384 | tf_op jit(solution)/shard_map/all_to_all | solution.py:29
  27.3 2.8 %shard_map.103 = (bf16[128,1024]{1,0:T(8,128)(2,1)S(1)}, f32[8,8,128]{2,1,0:T(8,128)S(1)}) custom-call(f32[8,2,128]{2,1,0:T(2,128)S(1)} %all_to_all.20.sums_ref, f32[128,1024]{1,0:T(8,128)S(1)} %get-tuple-element.26.mixed_ref, bf16[128,1024]{1,0:T(8,128)(2,1)S(1)} %get-tuple-element.23.query_ref, f32[128,1024]{1,0:T(8,128)S(1)} %get-tuple-element.24.scaled_ref, ...), custom_call_target="tpu_custom_call" | custom-call | flops 536870912 | bytes 2138112 | tf_op jit(solution)/shard_map/pallas_call | solution.py:41
  30.1 9.8 %all_to_all.21.parts_ref = f32[8,8,128]{2,1,0:T(8,128)S(1)} all-to-all(f32[8,8,128]{2,1,0:T(8,128)S(1)} %get-tuple-element.36), channel_id=1, replica_groups=mesh['far'=16,'near'=8,'chan'=8] {'near'}, dimensions={0} | all-to-all | bytes 65536 | tf_op jit(solution)/shard_map/all_to_all | solution.py:29
  39.9 0.6 shard_map.106
  40.5 30.4 %all-to-all-start.2 = ((bf16[16,8,128]{2,1,0:T(8,128)(2,1)}), bf16[16,8,128]{2,1,0:T(8,128)(2,1)S(1)}, u32[]{:S(2)}, u32[]{:S(2)}) async-start(bf16[16,8,128]{2,1,0:T(8,128)(2,1)} %shard_map.106), calls=%async_computation.2 | async-start | bytes 65536 | tf_op jit(solution)/shard_map/all_to_all | solution.py:29
  70.9 1.3 %collective-permute-start.1 = (bf16[128,1024]{1,0:T(8,128)(2,1)S(1)}, bf16[128,1024]{1,0:T(8,128)(2,1)S(1)}, u32[]{:S(2)}, u32[]{:S(2)}) collective-permute-start(bf16[128,1024]{1,0:T(8,128)(2,1)S(1)} %get-tuple-element.28.conv_ref), channel_id=1, source_target_pairs={{8,0},{16,8},{24,16},{32,24},{40,32},{48,40},{56,48},{64,56},{72,6... | collective-permute-start | bytes 786440 | tf_op jit(solution)/shard_map/ppermute | solution.py:23
  72.2 2.4 %all-to-all-done.2.parts_ref = bf16[16,8,128]{2,1,0:T(8,128)(2,1)S(1)} async-done(((bf16[16,8,128]{2,1,0:T(8,128)(2,1)}), bf16[16,8,128]{2,1,0:T(8,128)(2,1)S(1)}, u32[]{:S(2)}, u32[]{:S(2)}) %all-to-all-start.2) | async-done | bytes 32800 | tf_op jit(solution)/shard_map/all_to_all | solution.py:29
  74.6 0.6 shard_map.107
  75.3 3.3 %all-to-all-start.3 = ((f32[8,8,128]{2,1,0:T(8,128)}), f32[8,8,128]{2,1,0:T(8,128)S(1)}, u32[]{:S(2)}, u32[]{:S(2)}) async-start(f32[8,8,128]{2,1,0:T(8,128)} %shard_map.107), calls=%async_computation.3 | async-start | bytes 65536 | tf_op jit(solution)/shard_map/all_to_all | solution.py:29
  78.6 0.0 copy-done.3
  78.6 1.0 %shard_map.104 = (bf16[128,1024]{1,0:T(8,128)(2,1)}, bf16[128,1024]{1,0:T(8,128)(2,1)}) custom-call(f32[8,2,128]{2,1,0:T(2,128)S(1)} %all_to_all.20.sums_ref, f32[128,1024]{1,0:T(8,128)S(1)} %get-tuple-element.26.mixed_ref, bf16[128,1024]{1,0:T(8,128)(2,1)S(1)} %get-tuple-element.23.query_ref, f32[128,1024]{1,0:T(8,128)S(1)} %get-tuple-element.24.scaled_ref, ...), custom_call_target="tpu_custom_call" | custom-call | bytes 1847296 | tf_op jit(solution)/shard_map/pallas_call | solution.py:41
  79.6 0.0 collective-permute-done.1.after_ref
  79.7 0.0 copy-done
  79.7 0.0 copy-done.1
  79.7 0.0 copy-done.2
  79.7 2.1 %shard_map.105 = (bf16[128,1024]{1,0:T(8,128)(2,1)}, bf16[128,1024]{1,0:T(8,128)(2,1)}) custom-call(f32[64,128]{1,0:T(8,128)S(1)} %copy-done.2, bf16[128,1024]{1,0:T(8,128)(2,1)S(1)} %get-tuple-element.28.conv_ref, bf16[128,1024]{1,0:T(8,128)(2,1)S(1)} %collective-permute-done.1.after_ref, bf16[128,1024]{1,0:T(8,128)(2,1)S(1)} %bitcast.13, ...), custom_call_target="tpu_custom_call" | custom-call | flops 536870912 | bytes 1605632 | tf_op jit(solution)/shard_map/pallas_call | solution.py:41
  81.8 3.0 %all-to-all-done.3 = f32[8,8,128]{2,1,0:T(8,128)S(1)} async-done(((f32[8,8,128]{2,1,0:T(8,128)}), f32[8,8,128]{2,1,0:T(8,128)S(1)}, u32[]{:S(2)}, u32[]{:S(2)}) %all-to-all-start.3) | async-done | bytes 32800 | tf_op jit(solution)/shard_map/all_to_all | solution.py:29
  84.8 0.6 copy.12
Async XLA Ops:
  1.7 9.0 %collective-permute-start = (bf16[128,1024]{1,0:T(8,128)(2,1)S(1)}, bf16[128,1024]{1,0:T(8,128)(2,1)S(1)}, u32[]{:S(2)}, u32[]{:S(2)}) collective-permute-start(bf16[128,1024]{1,0:T(8,128)(2,1)S(1)} %multiply_convert_fusion.signal_ref), channel_id=1, source_target_pairs={{0,8},{8,16},{16,24},{24,32},{32,40},{40,48},{48,56},{56,64},{64,7... | collective-permute-start | bytes 786440 | tf_op jit(solution)/shard_map/ppermute | solution.py:23
  10.8 67.8 %copy-start.3 = (f32[1024]{0:T(1024)S(1)}, f32[1024]{0:T(1024)}, u32[]{:S(2)}) copy-start(f32[1024]{0:T(1024)} %param.11) | copy-start | bytes 12292
  11.6 68.0 %copy-start = (bf16[1,128,1024]{2,1,0:T(8,128)(2,1)S(1)}, bf16[1,128,1024]{2,1,0:T(8,128)(2,1)}, u32[]{:S(2)}) copy-start(bf16[1,128,1024]{2,1,0:T(8,128)(2,1)} %param.8) | copy-start | bytes 786436
  11.7 68.0 %copy-start.1 = (bf16[1,128,1024]{2,1,0:T(8,128)(2,1)S(1)}, bf16[1,128,1024]{2,1,0:T(8,128)(2,1)}, u32[]{:S(2)}) copy-start(bf16[1,128,1024]{2,1,0:T(8,128)(2,1)} %param.7) | copy-start | bytes 786436
  11.7 68.0 %copy-start.2 = (f32[64,128]{1,0:T(8,128)S(1)}, f32[64,128]{1,0:T(8,128)}, u32[]{:S(2)}) copy-start(f32[64,128]{1,0:T(8,128)} %filters_ref.3) | copy-start | bytes 98308
  40.5 34.1 %all-to-all-start.2 = ((bf16[16,8,128]{2,1,0:T(8,128)(2,1)}), bf16[16,8,128]{2,1,0:T(8,128)(2,1)S(1)}, u32[]{:S(2)}, u32[]{:S(2)}) async-start(bf16[16,8,128]{2,1,0:T(8,128)(2,1)} %shard_map.106), calls=%async_computation.2 | async-start | bytes 65536 | tf_op jit(solution)/shard_map/all_to_all | solution.py:29
  70.9 8.7 %collective-permute-start.1 = (bf16[128,1024]{1,0:T(8,128)(2,1)S(1)}, bf16[128,1024]{1,0:T(8,128)(2,1)S(1)}, u32[]{:S(2)}, u32[]{:S(2)}) collective-permute-start(bf16[128,1024]{1,0:T(8,128)(2,1)S(1)} %get-tuple-element.28.conv_ref), channel_id=1, source_target_pairs={{8,0},{16,8},{24,16},{32,24},{40,32},{48,40},{56,48},{64,56},{72,6... | collective-permute-start | bytes 786440 | tf_op jit(solution)/shard_map/ppermute | solution.py:23
  75.3 9.5 %all-to-all-start.3 = ((f32[8,8,128]{2,1,0:T(8,128)}), f32[8,8,128]{2,1,0:T(8,128)S(1)}, u32[]{:S(2)}, u32[]{:S(2)}) async-start(f32[8,8,128]{2,1,0:T(8,128)} %shard_map.107), calls=%async_computation.3 | async-start | bytes 65536 | tf_op jit(solution)/shard_map/all_to_all | solution.py:29
